TPU v7x, 32 devices: a whole 2x2x4 slice. The times are simulated.
32 devices in a mesh: dp: 8 (over z, x), tensor: 4 (over y, core).
Axes of the slice: x: 2, y: 2, z: 4, core: 2. Of those that a mesh axis runs over, the one named last changes fastest.
Arguments:
- embedded: bfloat16 [8192, 768], P(('dp', 'tensor')), may hold values from -6 to 6
- bigram_ids: int32 [8192], P(('dp', 'tensor')), may hold values from 0 to 16383, as said below
- trigram_ids: int32 [8192], P(('dp', 'tensor')), may hold values from 0 to 16383, as said below
- prefix_lens: int32 [8], P('dp'), may hold values from 102 to 512
- bigram_table: bfloat16 [16384, 192], P('dp'), may hold values from -6 to 6
- trigram_table: bfloat16 [16384, 192], P('dp'), may hold values from -6 to 6
- ngram_weight: bfloat16 [384, 768], replicated, may hold values from -0.3125 to 0.3125
- first_gain: float32 [768], replicated, may hold values from 0.5 to 1.5
- attend_weight: bfloat16 [768, 2304], P(None, 'tensor'), may hold values from -0.21875 to 0.21875
- output_weight: bfloat16 [768, 768], P('tensor'), may hold values from -0.875 to 0.875
- second_gain: float32 [768], replicated, may hold values from 0.5 to 1.5
- gate_weight: bfloat16 [768, 2048], P(None, 'tensor'), may hold values from -0.21875 to 0.21875
- up_weight: bfloat16 [768, 2048], P(None, 'tensor'), may hold values from -0.21875 to 0.21875
- down_weight: bfloat16 [2048, 768], P('tensor'), may hold values from -0.125 to 0.125
- cotangent: bfloat16 [8192, 768], P('dp'), may hold values from -6 to 6
Outputs:
- block_out: bfloat16 [8192, 768], P(('dp', 'tensor'))
- embed_grad: float32 [8192, 768], P(('dp', 'tensor'))
- bigram_grad: float32 [16384, 192], P(('dp', 'tensor'))
- trigram_grad: float32 [16384, 192], P(('dp', 'tensor'))
- ngram_weight_grad: float32 [384, 768], P(None, ('dp', 'tensor'))
- first_gain_grad: float32 [768], P(('dp', 'tensor'))
- attend_weight_grad: float32 [768, 2304], P('dp', 'tensor')
- output_weight_grad: float32 [768, 768], P('tensor', 'dp')
- second_gain_grad: float32 [768], P(('dp', 'tensor'))
- gate_weight_grad: float32 [768, 2048], P('dp', 'tensor')
- up_weight_grad: float32 [768, 2048], P('dp', 'tensor')
- down_weight_grad: float32 [2048, 768], P('tensor', 'dp')
Inputs may be any that keep to these rules, and one draw needn't show every extreme that they name: `bigram_ids`: row r of the 2-gram table is held by index r // 2048 of dp. Among the tokens of one device, at most 64 name rows of one holder; in every draw one holder gets exactly 64 from every device. `trigram_ids`: row r of the 3-gram table is held by index r // 2048 of dp. Among the tokens of one device, at most 64 name rows of one holder; in every draw one holder gets exactly 64 from every device.
All inputs are finite; a program needn't handle non-finite values.
Results may differ from a plain program's by a relative error of at most 0.022.
Values may be sent and summed in bfloat16 or wider, within the bound.
A program may use at most 128 MiB of HBM per device.

v0:
```python
import math

import jax
import jax.numpy as jnp
from jax import lax
from jax.sharding import PartitionSpec as P

HD = 64


def normed_rows(values_in, gain):
    scaling = lax.rsqrt(jnp.mean(values_in * values_in, axis=-1, keepdims=True) + 1e-05)
    return (values_in * scaling * gain, scaling)


def norm_backward(grad_out, values_in, scaling, gain):
    scaled = grad_out * gain
    gain_grad = jnp.sum(grad_out * values_in * scaling, axis=0)
    row_grad = scaling * scaled - values_in * scaling**3 * jnp.mean(
        scaled * values_in, axis=-1, keepdims=True
    )
    return (row_grad, gain_grad)


def rotary_tables(length, width):
    halfway = width // 2
    frequency = jnp.exp(jnp.arange(halfway, dtype=jnp.float32) * (-2.0 * math.log(10000.0) / width))
    angles = jnp.arange(length, dtype=jnp.float32)[:, None] * frequency[None, :]
    return (jnp.cos(angles), jnp.sin(angles))


def rotate(values_in, cosine, sines):
    halfway = values_in.shape[-1] // 2
    leading = values_in[..., :halfway]
    trailing = values_in[..., halfway:]
    cosine = cosine[:, None, :]
    sines = sines[:, None, :]
    return jnp.concatenate(
        [leading * cosine - trailing * sines, trailing * cosine + leading * sines], axis=-1
    )


def unrotate(grads, cosine, sines):
    halfway = grads.shape[-1] // 2
    leading = grads[..., :halfway]
    trailing = grads[..., halfway:]
    cosine = cosine[:, None, :]
    sines = sines[:, None, :]
    return jnp.concatenate(
        [leading * cosine + trailing * sines, trailing * cosine - leading * sines], axis=-1
    )


def inner(left, right):
    return lax.dot_general(
        left, right, (((0,), (0,)), ((), ())), preferred_element_type=jnp.float32
    )


def slot_positions(row_ids, rows_dev, peer_count, capacity):
    owner = row_ids // rows_dev
    onehot = (owner[:, None] == jnp.arange(peer_count)[None, :]).astype(jnp.float32)
    tokens = row_ids.shape[0]
    earlier = (jnp.arange(tokens)[None, :] < jnp.arange(tokens)[:, None]).astype(jnp.float32)
    ranks = jnp.dot(earlier, onehot, precision=lax.Precision.HIGHEST)
    slot = jnp.sum(ranks * onehot, axis=1).astype(jnp.int32)
    return owner * capacity + slot


def shards(
    embedded,
    bigram_ids,
    trigram_ids,
    prefix_lens,
    bigram_table,
    trigram_table,
    ngram_weight,
    first_gain,
    attend_weight,
    output_weight,
    second_gain,
    gate_weight,
    up_weight,
    down_weight,
    cotangent,
):
    peer_count = lax.axis_size("dp")
    split_count = lax.axis_size("tensor")
    local_rows = embedded.shape[0]
    length = local_rows * split_count
    rows_dev = bigram_table.shape[0]
    table_width = bigram_table.shape[1]
    capacity = max(4, 2 * local_rows // peer_count)
    scaling_factor = HD ** (-0.5)
    bigram_slot = slot_positions(bigram_ids, rows_dev, peer_count, capacity)
    trigram_slot = slot_positions(trigram_ids, rows_dev, peer_count, capacity)
    requests = jnp.zeros((2, peer_count * capacity), jnp.int32)
    requests = requests.at[0, bigram_slot].set(bigram_ids % rows_dev + 1)
    requests = requests.at[1, trigram_slot].set(trigram_ids % rows_dev + 1)
    requests = requests.reshape(2, peer_count, capacity)
    asked_rows = lax.all_to_all(requests, "dp", split_axis=1, concat_axis=1, tiled=True)
    picked = jnp.maximum(asked_rows - 1, 0)
    found_rows = jnp.stack([bigram_table[picked[0]], trigram_table[picked[1]]])
    answer = lax.all_to_all(found_rows, "dp", split_axis=1, concat_axis=1, tiled=True)
    fetched, asked_rows = (answer, asked_rows)
    fetched = fetched.reshape(2, peer_count * capacity, table_width)
    ngram_rows = jnp.concatenate([fetched[0][bigram_slot], fetched[1][trigram_slot]], axis=1)
    lifted = jnp.dot(ngram_rows, ngram_weight, preferred_element_type=jnp.float32)
    inputs = embedded.astype(jnp.float32) + lifted
    normed_one, first_scale = normed_rows(inputs, first_gain)
    normed_one_full = lax.all_gather(normed_one.astype(jnp.bfloat16), "tensor", axis=0, tiled=True)
    head_count = attend_weight.shape[1] // (3 * HD)
    mixture = jnp.dot(normed_one_full, attend_weight, preferred_element_type=jnp.float32)
    mixture = mixture.reshape(length, head_count, 3, HD)
    cosine, sines = rotary_tables(length, HD)
    queries = rotate(mixture[:, :, 0], cosine, sines).astype(jnp.bfloat16)
    keys = rotate(mixture[:, :, 1], cosine, sines).astype(jnp.bfloat16)
    values = mixture[:, :, 2].astype(jnp.bfloat16)
    block_size = min(512, length)
    block_count = length // block_size
    prefix = prefix_lens[0]
    key_position = jnp.arange(length)

    def scores_of(query_block, offset):
        products = (
            jnp.einsum("qhd,khd->hqk", query_block, keys, preferred_element_type=jnp.float32)
            * scaling_factor
        )
        query_position = offset + jnp.arange(block_size)
        allowed = (key_position[None, :] <= query_position[:, None]) | (
            key_position[None, :] < prefix
        )
        return jnp.where(allowed[None], products, -1000000000.0)

    def forward_block(position):
        offset = position * block_size
        query_block = lax.dynamic_slice_in_dim(queries, offset, block_size, 0)
        scores = scores_of(query_block, offset)
        highest_score = jnp.max(scores, axis=-1, keepdims=True)
        powers = jnp.exp(scores - highest_score)
        totals = jnp.sum(powers, axis=-1, keepdims=True)
        weights_low = (powers / totals).astype(jnp.bfloat16)
        result = jnp.einsum("hqk,khd->qhd", weights_low, values, preferred_element_type=jnp.float32)
        return (result.astype(jnp.bfloat16), (highest_score + jnp.log(totals))[..., 0])

    attended, log_totals = lax.map(forward_block, jnp.arange(block_count))
    attended = attended.reshape(length, head_count * HD)
    part_rows = attended
    branch_one = lax.psum_scatter(
        jnp.dot(part_rows, output_weight, preferred_element_type=jnp.float32).astype(jnp.bfloat16),
        "tensor",
        scatter_dimension=0,
        tiled=True,
    ).astype(jnp.float32)
    after = inputs + branch_one
    normed_two, second_scale = normed_rows(after, second_gain)
    normed_two_full = lax.all_gather(normed_two.astype(jnp.bfloat16), "tensor", axis=0, tiled=True)
    gate = jnp.dot(normed_two_full, gate_weight, preferred_element_type=jnp.float32)
    up_part = jnp.dot(normed_two_full, up_weight, preferred_element_type=jnp.float32)
    sigmoid_gate = jax.nn.sigmoid(gate)
    activity = (gate * sigmoid_gate * up_part).astype(jnp.bfloat16)
    part_rows = activity
    branch_two = lax.psum_scatter(
        jnp.dot(part_rows, down_weight, preferred_element_type=jnp.float32).astype(jnp.bfloat16),
        "tensor",
        scatter_dimension=0,
        tiled=True,
    ).astype(jnp.float32)
    block_out = (after + branch_two).astype(jnp.bfloat16)
    own_cot = lax.dynamic_slice_in_dim(
        cotangent, lax.axis_index("tensor") * local_rows, local_rows, 0
    ).astype(jnp.float32)
    down_grad = inner(activity, cotangent)
    activity_back = jnp.dot(cotangent, down_weight.T, preferred_element_type=jnp.float32)
    gate_back = (
        activity_back * up_part * sigmoid_gate * (1.0 + gate * (1.0 - sigmoid_gate))
    ).astype(jnp.bfloat16)
    up_back = (activity_back * gate * sigmoid_gate).astype(jnp.bfloat16)
    gate_grad = inner(normed_two_full, gate_back)
    up_grad = inner(normed_two_full, up_back)
    normed_two_back = lax.psum_scatter(
        (
            jnp.dot(gate_back, gate_weight.T, preferred_element_type=jnp.float32)
            + jnp.dot(up_back, up_weight.T, preferred_element_type=jnp.float32)
        ).astype(jnp.bfloat16),
        "tensor",
        scatter_dimension=0,
        tiled=True,
    ).astype(jnp.float32)
    second_row_grad, second_partial = norm_backward(
        normed_two_back, after, second_scale, second_gain
    )
    after_grad = own_cot + second_row_grad
    attn_back_full = lax.all_gather(after_grad.astype(jnp.bfloat16), "tensor", axis=0, tiled=True)
    output_grad = inner(attended, attn_back_full)
    attended_back = jnp.dot(
        attn_back_full, output_weight.T, preferred_element_type=jnp.float32
    ).astype(jnp.bfloat16)
    attended_back = attended_back.reshape(length, head_count, HD)

    def backward_block(carry, item):
        key_sum, value_sum = carry
        position, log_block = item
        offset = position * block_size
        query_block = lax.dynamic_slice_in_dim(queries, offset, block_size, 0)
        grad_block = lax.dynamic_slice_in_dim(attended_back, offset, block_size, 0)
        probs = jnp.exp(scores_of(query_block, offset) - log_block[..., None])
        prob_back = jnp.einsum(
            "qhd,khd->hqk", grad_block, values, preferred_element_type=jnp.float32
        )
        centre = jnp.sum(probs * prob_back, axis=-1, keepdims=True)
        score_back = (probs * (prob_back - centre)).astype(jnp.bfloat16)
        query_grad = (
            jnp.einsum("hqk,khd->qhd", score_back, keys, preferred_element_type=jnp.float32)
            * scaling_factor
        )
        key_sum = (
            key_sum
            + jnp.einsum(
                "hqk,qhd->khd", score_back, query_block, preferred_element_type=jnp.float32
            )
            * scaling_factor
        )
        value_sum = value_sum + jnp.einsum(
            "hqk,qhd->khd",
            probs.astype(jnp.bfloat16),
            grad_block,
            preferred_element_type=jnp.float32,
        )
        return ((key_sum, value_sum), query_grad)

    zero_heads = jnp.zeros((length, head_count, HD), jnp.float32)
    (key_sum, value_sum), query_grads = lax.scan(
        backward_block, (zero_heads, zero_heads), (jnp.arange(block_count), log_totals)
    )
    query_back = (
        query_grads.reshape(length, head_count, HD).astype(jnp.bfloat16).astype(jnp.float32)
    )
    key_back = key_sum.astype(jnp.bfloat16).astype(jnp.float32)
    mixture_back = jnp.stack(
        [unrotate(query_back, cosine, sines), unrotate(key_back, cosine, sines), value_sum], axis=2
    )
    mixture_back = mixture_back.reshape(length, head_count * 3 * HD).astype(jnp.bfloat16)
    attend_grad = inner(normed_one_full, mixture_back)
    part_rows = mixture_back
    normed_one_back = lax.psum_scatter(
        jnp.dot(part_rows, attend_weight.T, preferred_element_type=jnp.float32).astype(
            jnp.bfloat16
        ),
        "tensor",
        scatter_dimension=0,
        tiled=True,
    ).astype(jnp.float32)
    first_row_grad, first_partial = norm_backward(normed_one_back, inputs, first_scale, first_gain)
    embed_grad = after_grad + first_row_grad
    lifted_back = embed_grad.astype(jnp.bfloat16)
    ngram_partial = inner(ngram_rows, lifted_back)
    row_back = jnp.dot(lifted_back, ngram_weight.T, preferred_element_type=jnp.float32)
    outgoing = jnp.zeros((2, peer_count * capacity, table_width), jnp.float32)
    outgoing = outgoing.at[0, bigram_slot].set(row_back[:, :table_width])
    outgoing = outgoing.at[1, trigram_slot].set(row_back[:, table_width:])
    outgoing = outgoing.reshape(2, peer_count, capacity, table_width)
    arrived = lax.all_to_all(
        outgoing.astype(jnp.bfloat16), "dp", split_axis=1, concat_axis=1, tiled=True
    ).astype(outgoing.dtype)
    picked_rows = jnp.maximum(asked_rows - 1, 0)
    bigram_part = (
        jnp.zeros((rows_dev, table_width), jnp.float32)
        .at[picked_rows[0].reshape(-1)]
        .add(arrived[0].reshape(-1, table_width))
    )
    trigram_part = (
        jnp.zeros((rows_dev, table_width), jnp.float32)
        .at[picked_rows[1].reshape(-1)]
        .add(arrived[1].reshape(-1, table_width))
    )
    attend_sum, output_sum, gate_sum, up_sum, down_sum, ngram_group, first_group, second_group = (
        lax.psum_scatter(attend_grad, "dp", scatter_dimension=0, tiled=True),
        lax.psum_scatter(output_grad, "dp", scatter_dimension=1, tiled=True),
        lax.psum_scatter(gate_grad, "dp", scatter_dimension=0, tiled=True),
        lax.psum_scatter(up_grad, "dp", scatter_dimension=0, tiled=True),
        lax.psum_scatter(down_grad, "dp", scatter_dimension=1, tiled=True),
        lax.psum_scatter(ngram_partial, "dp", scatter_dimension=1, tiled=True),
        lax.psum_scatter(first_partial, "dp", scatter_dimension=0, tiled=True),
        lax.psum_scatter(second_partial, "dp", scatter_dimension=0, tiled=True),
    )
    bigram_grad, trigram_grad, ngram_grad, first_grad, second_grad = (
        lax.psum_scatter(
            bigram_part.astype(jnp.bfloat16), "tensor", scatter_dimension=0, tiled=True
        ).astype(jnp.float32),
        lax.psum_scatter(
            trigram_part.astype(jnp.bfloat16), "tensor", scatter_dimension=0, tiled=True
        ).astype(jnp.float32),
        lax.psum_scatter(
            ngram_group.astype(jnp.bfloat16), "tensor", scatter_dimension=1, tiled=True
        ).astype(jnp.float32),
        lax.psum_scatter(
            first_group.astype(jnp.bfloat16), "tensor", scatter_dimension=0, tiled=True
        ).astype(jnp.float32),
        lax.psum_scatter(
            second_group.astype(jnp.bfloat16), "tensor", scatter_dimension=0, tiled=True
        ).astype(jnp.float32),
    )
    return (
        block_out,
        embed_grad,
        bigram_grad,
        trigram_grad,
        ngram_grad,
        first_grad,
        attend_sum,
        output_sum,
        second_grad,
        gate_sum,
        up_sum,
        down_sum,
    )


def solution(mesh):
    placed = (
        P(("dp", "tensor"), None),
        P(("dp", "tensor")),
        P(("dp", "tensor")),
        P("dp"),
        P("dp", None),
        P("dp", None),
        P(),
        P(),
        P(None, "tensor"),
        P("tensor", None),
        P(),
        P(None, "tensor"),
        P(None, "tensor"),
        P("tensor", None),
        P("dp", None),
    )
    return jax.shard_map(
        shards,
        mesh=mesh,
        in_specs=placed,
        out_specs=(
            P(("dp", "tensor"), None),
            P(("dp", "tensor"), None),
            P(("dp", "tensor"), None),
            P(("dp", "tensor"), None),
            P(None, ("dp", "tensor")),
            P(("dp", "tensor")),
            P("dp", "tensor"),
            P("tensor", "dp"),
            P(("dp", "tensor")),
            P("dp", "tensor"),
            P("dp", "tensor"),
            P("tensor", "dp"),
        ),
        check_vma=False,
    )
```

profile of v0, /device:TPU:0, one launch (start us, length us, event | category | flops | bytes accessed | tf_op | source)
XLA Modules:
  0.0 817.4 jit_solution(4274439268550508631)
XLA Ops:
  9.2 12.4 %scatter_fusion = s32[2,512]{1,0:T(2,128)S(1)} fusion(s32[2,512]{1,0:T(2,128)S(1)} %broadcast_in_dim.44, s32[256]{0:T(256)S(1)} %bitcast.157, s32[256]{0:T(256)S(1)} %get-tuple-element.362), kind=kCustom, calls=%fused_computation.4 | custom fusion | bytes 5120 | tf_op jit(solution)/shard_map/scatter | solution.py:98
  21.6 12.4 %scatter_fusion.1 = s32[2,512]{1,0:T(2,128)S(1)} fusion(s32[2,512]{1,0:T(2,128)S(1)} %scatter_fusion, s32[256]{0:T(256)S(1)} %bitcast.159, s32[256]{0:T(256)S(1)} %get-tuple-element.360), kind=kCustom, calls=%fused_computation.5 | custom fusion | bytes 5120 | tf_op jit(solution)/shard_map/scatter | solution.py:99
  34.7 7.3 all-to-all-start
  58.9 13.2 %all-to-all-done.1 = bf16[2,8,64,192]{3,2,0,1:T(8,128)(2,1)S(1)} async-done(((bf16[2,8,64,192]{3,2,0,1:T(8,128)(2,1)}), bf16[2,8,64,192]{3,2,0,1:T(8,128)(2,1)S(1)}, u32[]{:S(2)}, u32[]{:S(2)}) %all-to-all-start.1) | async-done | bytes 393248 | tf_op jit(solution)/shard_map/all_to_all | solution.py:104
  77.3 18.1 %all-gather.4.cloned.1.call-done = bf16[1024,768]{1,0:T(8,128)(2,1)} async-done(((bf16[256,768]{1,0:T(8,128)(2,1)}), bf16[1024,768]{1,0:T(8,128)(2,1)}) %all-gather.4.cloned.1.call-update) | async-done | bytes 1572880 | tf_op jit(solution)/shard_map/all_gather | solution.py:111
  98.7 15.5 %while.30 = (s32[]{:T(128)}, bf16[2,512,3,64]{1,3,2,0:T(8,128)(2,1)S(1)}, f32[2,3,512]{2,1,0:T(4,128)S(1)}, s32[2]{0:T(128)S(1)}, s32[]{:T(128)}, /*index=5*/bf1...) while((s32[]{:T(128)}, ...), condition=%wide.region_8.9_spmd.clone.clone, body=%wide.region_5.8_spmd.clone.clone.sunk | while | flops 422674432 | bytes 22216908 | solution.py:146
  118.4 28.3 %reduce-scatter.18.cloned.1.call-done = bf16[256,768]{1,0:T(8,128)(2,1)} async-done(((bf16[1024,768]{1,0:T(8,128)(2,1)}), bf16[256,768]{1,0:T(8,128)(2,1)}) %reduce-scatter.18.cloned.1.call-update) | async-done | bytes 393232 | tf_op jit(solution)/shard_map/reduce_scatter | solution.py:149
  150.4 19.8 %all-gather.6.cloned.1.call-done = bf16[1024,768]{1,0:T(8,128)(2,1)} async-done(((bf16[256,768]{1,0:T(8,128)(2,1)}), bf16[1024,768]{1,0:T(8,128)(2,1)}) %all-gather.6.cloned.1.call-update) | async-done | bytes 1572880 | tf_op jit(solution)/shard_map/all_gather | solution.py:157
  181.3 28.3 %reduce-scatter.22.cloned.1.call-done = bf16[256,768]{1,0:T(8,128)(2,1)} async-done(((bf16[1024,768]{1,0:T(8,128)(2,1)}), bf16[256,768]{1,0:T(8,128)(2,1)}) %reduce-scatter.22.cloned.1.call-update) | async-done | bytes 393232 | tf_op jit(solution)/shard_map/reduce_scatter | solution.py:181
  213.9 19.5 %all-gather.8.cloned.1.call-done = bf16[1024,768]{1,0:T(8,128)(2,1)} async-done(((bf16[256,768]{1,0:T(8,128)(2,1)}), bf16[1024,768]{1,0:T(8,128)(2,1)}) %all-gather.8.cloned.1.call-update) | async-done | bytes 1572880 | tf_op jit(solution)/shard_map/all_gather | solution.py:194
  236.3 23.7 %while.31 = (s32[]{:T(128)}, f32[1024,3,64]{0,2,1:T(8,128)S(1)}, f32[1024,3,64]{0,2,1:T(8,128)}, bf16[2,512,3,64]{1,3,2,0:T(8,128)(2,1)}, s32[2]{0:T(128)S(1)}, ...) while((s32[]{:T(128)}, f32[1024,3,64]{0,2,1:T(8,128)S(1)}, ...), condition=%wide.region_16.17_spmd.clone.clone, body=%wide.region_14.16_spmd.clone.clone.sunk | while | flops 1032355840 | bytes 67424672 | solution.py:233
  269.2 25.6 %reduce-scatter.24.cloned.1.call-done = bf16[256,768]{1,0:T(8,128)(2,1)} async-done(((bf16[1024,768]{1,0:T(8,128)(2,1)}), bf16[256,768]{1,0:T(8,128)(2,1)}) %reduce-scatter.24.cloned.1.call-update) | async-done | bytes 393232 | tf_op jit(solution)/shard_map/reduce_scatter | solution.py:246
  296.0 29.6 %reduce-scatter.20.cloned.1.call-done = bf16[256,768]{1,0:T(8,128)(2,1)} async-done(((bf16[1024,768]{1,0:T(8,128)(2,1)}), bf16[256,768]{1,0:T(8,128)(2,1)}) %reduce-scatter.20.cloned.1.call-update) | async-done | bytes 393232 | tf_op jit(solution)/shard_map/reduce_scatter | solution.py:163
  333.6 13.1 %scatter_fusion.2 = f32[2,512,192]{2,1,0:T(8,128)S(1)} fusion(f32[2,512,192]{2,1,0:T(8,128)S(1)} %broadcast_in_dim.58, s32[256]{0:T(256)S(1)} %bitcast.158, f32[256,192]{1,0:T(8,128)S(1)} %get-tuple-element.347), kind=kCustom, calls=%fused_computation.6 | custom fusion | bytes 591872 | tf_op jit(solution)/shard_map/scatter | solution.py:260
  346.7 13.1 %scatter_fusion.3 = f32[2,512,192]{2,1,0:T(8,128)S(1)} fusion(f32[2,512,192]{2,1,0:T(8,128)S(1)} %scatter_fusion.2, s32[256]{0:T(256)S(1)} %bitcast.160, f32[256,192]{1,0:T(8,128)S(1)} %get-tuple-element.346), kind=kCustom, calls=%fused_computation.7 | custom fusion | bytes 591872 | tf_op jit(solution)/shard_map/scatter | solution.py:261
  366.4 14.3 %all-to-all-done.2 = bf16[2,8,64,192]{3,2,0,1:T(8,128)(2,1)S(1)} async-done(((bf16[2,8,64,192]{3,2,0,1:T(8,128)(2,1)}), bf16[2,8,64,192]{3,2,0,1:T(8,128)(2,1)S(1)}, u32[]{:S(2)}, u32[]{:S(2)}) %all-to-all-start.2) | async-done | bytes 393248 | tf_op jit(solution)/shard_map/all_to_all | solution.py:263
  415.0 45.6 %reduce-scatter.40.cloned.1.call-done = f32[96,192]{1,0:T(8,128)} async-done(((f32[768,192]{1,0:T(8,128)}), f32[96,192]{1,0:T(8,128)}) %reduce-scatter.40.cloned.1.call-update) | async-done | bytes 73744
  462.2 19.6 %all-reduce.7 = (bf16[768]{0:T(1024)(128)(2,1)S(1)}, bf16[768]{0:T(1024)(128)(2,1)S(1)}) all-reduce(f32[768]{0:T(1024)S(1)} %get-tuple-element.279, f32[768]{0:T(1024)S(1)} %copy-done.50), channel_id=10, replica_groups=mesh['dp'=8,'tensor'=4] {'dp'}, use_global_device_ids=true, to_apply=%region_28.29.clone | all-reduce | flops 1536 | bytes 9216
  490.6 24.0 %reduce-scatter.28.cloned.1.call-done = bf16[512,192]{1,0:T(8,128)(2,1)} async-done(((bf16[2048,192]{1,0:T(8,128)(2,1)}), bf16[512,192]{1,0:T(8,128)(2,1)}) %reduce-scatter.28.cloned.1.call-update) | async-done | bytes 196624 | tf_op jit(solution)/shard_map/reduce_scatter | solution.py:291
  516.5 19.7 %reduce-scatter.42.cloned.1.call-done = bf16[384,24]{0,1:T(8,128)(2,1)} async-done(((bf16[384,96]{0,1:T(8,128)(2,1)}), bf16[384,24]{0,1:T(8,128)(2,1)}) %reduce-scatter.42.cloned.1.call-update) | async-done | bytes 18448
  537.5 67.9 %reduce-scatter.34.cloned.1.call-done = f32[96,512]{1,0:T(8,128)} async-done(((f32[768,512]{1,0:T(8,128)}), f32[96,512]{1,0:T(8,128)}) %reduce-scatter.34.cloned.1.call-update) | async-done | bytes 196624 | tf_op jit(solution)/shard_map/reduce_scatter | solution.py:280
  605.4 67.6 %reduce-scatter.36.cloned.1.call-done = f32[96,512]{1,0:T(8,128)} async-done(((f32[768,512]{1,0:T(8,128)}), f32[96,512]{1,0:T(8,128)}) %reduce-scatter.36.cloned.1.call-update) | async-done | bytes 196624 | tf_op jit(solution)/shard_map/reduce_scatter | solution.py:281
  673.0 68.0 %reduce-scatter.38.cloned.1.call-done = f32[512,96]{0,1:T(8,128)} async-done(((f32[512,768]{0,1:T(8,128)}), f32[512,96]{0,1:T(8,128)}) %reduce-scatter.38.cloned.1.call-update) | async-done | bytes 196624 | tf_op jit(solution)/shard_map/reduce_scatter | solution.py:282
  741.0 69.7 %reduce-scatter.32.cloned.1.call-done = f32[96,576]{1,0:T(8,128)} async-done(((f32[768,576]{1,0:T(8,128)}), f32[96,576]{1,0:T(8,128)}) %reduce-scatter.32.cloned.1.call-update) | async-done | bytes 221200 | tf_op jit(solution)/shard_map/reduce_scatter | solution.py:278
  (329 shorter events, 160.9 us)
Async XLA Ops:
  7.2 88.3 %copy-start = (bf16[768,576]{0,1:T(8,128)(2,1)S(1)}, bf16[768,576]{0,1:T(8,128)(2,1)}, u32[]{:S(2)}) copy-start(bf16[768,576]{0,1:T(8,128)(2,1)} %param.27) | copy-start | bytes 2654212
  34.7 13.7 %all-to-all-start = ((s32[8,1,128]{2,1,0:T(1,128)}), s32[8,1,128]{2,1,0:T(1,128)S(1)}, u32[]{:S(2)}, u32[]{:S(2)}) async-start(s32[8,1,128]{2,1,0:T(1,128)} %reshape.467), calls=%async_computation | async-start | bytes 8192 | tf_op jit(solution)/shard_map/all_to_all | solution.py:101
  55.2 16.9 %all-to-all-start.1 = ((bf16[2,8,64,192]{3,2,0,1:T(8,128)(2,1)}), bf16[2,8,64,192]{3,2,0,1:T(8,128)(2,1)S(1)}, u32[]{:S(2)}, u32[]{:S(2)}) async-start(bf16[2,8,64,192]{3,2,0,1:T(8,128)(2,1)} %pad_maximum_fusion.1), calls=%async_computation.1 | async-start | bytes 1048576 | tf_op jit(solution)/shard_map/all_to_all | solution.py:104
  58.9 36.6 %all-gather.4.cloned.1.call-start = ((), (), s32[]{:S(2)}) async-start(), calls=%async_computation.16 | async-start | bytes 1966080 | tf_op jit(solution)/shard_map/all_gather | solution.py:111
  76.5 70.1 %reduce-scatter.18.cloned.1.call-start = ((), (), s32[]{:S(2)}) async-start(), calls=%async_computation.17 | async-start | bytes 1966080 | tf_op jit(solution)/shard_map/reduce_scatter | solution.py:149
  118.3 51.8 %all-gather.6.cloned.1.call-start = ((), (), s32[]{:S(2)}) async-start(), calls=%async_computation.18 | async-start | bytes 1966080 | tf_op jit(solution)/shard_map/all_gather | solution.py:157
  150.3 59.2 %reduce-scatter.22.cloned.1.call-start = ((), (), s32[]{:S(2)}) async-start(), calls=%async_computation.20 | async-start | bytes 1966080 | tf_op jit(solution)/shard_map/reduce_scatter | solution.py:181
  181.2 52.3 %all-gather.8.cloned.1.call-start = ((), (), s32[]{:S(2)}) async-start(), calls=%async_computation.21 | async-start | bytes 1966080 | tf_op jit(solution)/shard_map/all_gather | solution.py:194
  213.6 81.1 %reduce-scatter.24.cloned.1.call-start = ((), (), s32[]{:S(2)}) async-start(), calls=%async_computation.22 | async-start | bytes 1966080 | tf_op jit(solution)/shard_map/reduce_scatter | solution.py:246
  266.4 59.2 %reduce-scatter.20.cloned.1.call-start = ((), (), s32[]{:S(2)}) async-start(), calls=%async_computation.19 | async-start | bytes 1966080 | tf_op jit(solution)/shard_map/reduce_scatter | solution.py:163
  268.7 57.0 %copy-start.49 = (f32[256]{0:T(256)S(1)}, f32[256]{0:T(256)}, u32[]{:S(2)}) copy-start(f32[256]{0:T(256)} %copy-done.47) | copy-start | bytes 3076
  268.7 57.0 %copy-start.54 = (f32[256]{0:T(256)S(1)}, f32[256]{0:T(256)}, u32[]{:S(2)}) copy-start(f32[256]{0:T(256)} %get-tuple-element.358) | copy-start | bytes 3076
  268.7 57.0 %copy-start.56 = (f32[256]{0:T(256)S(1)}, f32[256]{0:T(256)}, u32[]{:S(2)}) copy-start(f32[256]{0:T(256)} %copy-done.55) | copy-start | bytes 3076
  268.7 57.0 %copy-start.57 = (f32[256]{0:T(256)S(1)}, f32[256]{0:T(256)}, u32[]{:S(2)}) copy-start(f32[256]{0:T(256)} %get-tuple-element.356) | copy-start | bytes 3076
  268.7 127.1 %reduce-scatter.30.cloned.1.call-start = ((), (), s32[]{:S(2)}) async-start(), calls=%async_computation.25 | async-start | bytes 1327104 | tf_op jit(solution)/shard_map/reduce_scatter | solution.py:283
  329.7 130.9 %reduce-scatter.40.cloned.1.call-start = ((), (), s32[]{:S(2)}) async-start(), calls=%async_computation.30 | async-start | bytes 884736
  360.8 20.0 %all-to-all-start.2 = ((bf16[2,8,64,192]{3,2,0,1:T(8,128)(2,1)}), bf16[2,8,64,192]{3,2,0,1:T(8,128)(2,1)S(1)}, u32[]{:S(2)}, u32[]{:S(2)}) async-start(bf16[2,8,64,192]{3,2,0,1:T(8,128)(2,1)} %copy.69), calls=%async_computation.6 | async-start | bytes 1048576 | tf_op jit(solution)/shard_map/all_to_all | solution.py:263
  366.3 122.5 %reduce-scatter.26.cloned.1.call-start = ((), (), s32[]{:S(2)}) async-start(), calls=%async_computation.23 | async-start | bytes 1310720 | tf_op jit(solution)/shard_map/reduce_scatter | solution.py:288
  387.4 127.3 %reduce-scatter.28.cloned.1.call-start = ((), (), s32[]{:S(2)}) async-start(), calls=%async_computation.24 | async-start | bytes 1310720 | tf_op jit(solution)/shard_map/reduce_scatter | solution.py:291
  392.7 143.5 %reduce-scatter.42.cloned.1.call-start = ((), (), s32[]{:S(2)}) async-start(), calls=%async_computation.31 | async-start | bytes 92160
  397.4 208.0 %reduce-scatter.34.cloned.1.call-start = ((), (), s32[]{:S(2)}) async-start(), calls=%async_computation.27 | async-start | bytes 1769472 | tf_op jit(solution)/shard_map/reduce_scatter | solution.py:280
  401.6 271.4 %reduce-scatter.36.cloned.1.call-start = ((), (), s32[]{:S(2)}) async-start(), calls=%async_computation.28 | async-start | bytes 1769472 | tf_op jit(solution)/shard_map/reduce_scatter | solution.py:281
  403.9 337.2 %reduce-scatter.38.cloned.1.call-start = ((), (), s32[]{:S(2)}) async-start(), calls=%async_computation.29 | async-start | bytes 1769472 | tf_op jit(solution)/shard_map/reduce_scatter | solution.py:282
  408.3 402.4 %reduce-scatter.32.cloned.1.call-start = ((), (), s32[]{:S(2)}) async-start(), calls=%async_computation.26 | async-start | bytes 2211840 | tf_op jit(solution)/shard_map/reduce_scatter | solution.py:278
  (66 other events, 887.6 us)
Sparse Core Ops, SparseCore 0:
  76.6 18.7 all-gather.3
  118.4 28.1 reduce-scatter.17
  150.5 19.6 all-gather.5
  181.3 28.1 reduce-scatter.21
  213.8 19.6 all-gather.7
  266.6 28.1 reduce-scatter.23
  297.4 28.1 reduce-scatter.19
  329.8 65.9 reduce-scatter.29
  399.1 61.4 reduce-scatter.39
  463.1 23.9 reduce-scatter.25
  489.6 24.9 reduce-scatter.27
  517.1 19.0 reduce-scatter.41
  540.6 64.8 reduce-scatter.33
  609.3 63.7 reduce-scatter.35
  677.3 63.7 reduce-scatter.37
  745.0 65.7 reduce-scatter.31
where the time goes:
time: 823 us; the launch traced here: 817 us
  waiting for transfers between devices  567 us (69%)
  local copies, waits for them, and re-layouts  77.9 us (9%)
  matrix products  64.9 us (8%)
  other arithmetic  45 us (5%)
  blocking collectives  25.3 us (3%)
  starting transfers between devices  18 us (2%)
  between operations  16.4 us (2%)
    reduce_scatter x1, waiting for transfers between devices, shards(): lax.psum_scatter(attend_grad, 'dp', scatter_dimension=0, tiled=True)  69.7 us
    reduce_scatter x1, waiting for transfers between devices, shards(): lax.psum_scatter(down_grad, 'dp', scatter_dimension=1, tiled=True)  68 us
    reduce_scatter x1, waiting for transfers between devices, shards(): lax.psum_scatter(gate_grad, 'dp', scatter_dimension=0, tiled=True)  67.9 us
    reduce_scatter x1, waiting for transfers between devices, shards(): lax.psum_scatter(up_grad, 'dp', scatter_dimension=0, tiled=True)  67.6 us
    unnamed x18, waiting for transfers between devices  65.6 us
    reduce_scatter x1, waiting for transfers between devices, shards(): lax.psum_scatter(jnp.dot(part_rows, down_weight, preferred_element_type=j...  29.6 us
    reduce_scatter x1, waiting for transfers between devices, shards(): lax.psum_scatter((jnp.dot(gate_back, gate_weight.T, preferred_element_typ...  28.3 us
    reduce_scatter x1, waiting for transfers between devices, shards(): lax.psum_scatter(jnp.dot(part_rows, output_weight, preferred_element_type...  28.3 us
  transfers between devices with their start and end apart: 19, of which 18 were waited for; matrix products, arithmetic and copies ran while one was open for 9% of the time, Pallas kernels for 0%

commit v1 on v0

--- a/solution.py
+++ b/solution.py
@@ -1,8 +1,11 @@
+import functools
 import math
 
 import jax
 import jax.numpy as jnp
 from jax import lax
+from jax.experimental import pallas as pl
+from jax.experimental.pallas import tpu as pltpu
 from jax.sharding import PartitionSpec as P
 
 HD = 64
@@ -55,6 +58,80 @@
     return lax.dot_general(
         left, right, (((0,), (0,)), ((), ())), preferred_element_type=jnp.float32
     )
+
+
+def reduce_kernel(peers, part_ref, out_ref, mine, pair_in, pair_out, far_in, sems):
+    groups = peers // 2
+    me = lax.axis_index("dp")
+    parity = lax.rem(me, 2)
+    place = me // 2
+    partner = me + 1 - 2 * parity
+    barrier = pltpu.get_barrier_semaphore()
+    pl.semaphore_signal(barrier, inc=1, device_id={"dp": partner})
+    for step in range(1, groups):
+        target = lax.rem(place + step, groups) * 2 + parity
+        pl.semaphore_signal(barrier, inc=1, device_id={"dp": target})
+    pl.semaphore_wait(barrier, groups)
+    near = []
+    for step in range(1, groups + 1):
+        group = lax.rem(place + step, groups)
+        copy = pltpu.make_async_remote_copy(
+            src_ref=part_ref.at[group * 2 + 1 - parity],
+            dst_ref=pair_in.at[group],
+            send_sem=sems.at[0, step - 1],
+            recv_sem=sems.at[1, step - 1],
+            device_id={"dp": partner},
+        )
+        copy.start()
+        near.append(copy)
+    own = pltpu.make_async_copy(part_ref, mine, sems.at[4, 0])
+    own.start()
+    own.wait()
+    far = []
+    for step in range(1, groups + 1):
+        group = lax.rem(place + step, groups)
+        near[step - 1].wait_recv()
+        total = mine[group * 2 + parity].astype(jnp.float32) + pair_in[group].astype(jnp.float32)
+        if step == groups:
+            out_ref[...] = total
+            break
+        pair_out[step - 1] = total.astype(jnp.bfloat16)
+        copy = pltpu.make_async_remote_copy(
+            src_ref=pair_out.at[step - 1],
+            dst_ref=far_in.at[step - 1],
+            send_sem=sems.at[2, step - 1],
+            recv_sem=sems.at[3, step - 1],
+            device_id={"dp": group * 2 + parity},
+        )
+        copy.start()
+        far.append(copy)
+    for step, copy in enumerate(far):
+        copy.wait_recv()
+        out_ref[...] += far_in[step].astype(jnp.float32)
+    for copy in near + far:
+        copy.wait_send()
+
+
+def reduce_over_dp(parts):
+    peers, rows, width = parts.shape
+    groups = peers // 2
+    return pl.pallas_call(
+        functools.partial(reduce_kernel, peers),
+        out_shape=jax.ShapeDtypeStruct((rows, width), jnp.float32),
+        in_specs=[pl.BlockSpec(memory_space=pl.ANY)],
+        out_specs=pl.BlockSpec(memory_space=pltpu.VMEM),
+        scratch_shapes=[
+            pltpu.VMEM((peers, rows, width), jnp.bfloat16),
+            pltpu.VMEM((groups, rows, width), jnp.bfloat16),
+            pltpu.VMEM((groups - 1, rows, width), jnp.bfloat16),
+            pltpu.VMEM((groups - 1, rows, width), jnp.bfloat16),
+            pltpu.SemaphoreType.DMA((5, groups)),
+        ],
+        compiler_params=pltpu.CompilerParams(
+            collective_id=0, has_side_effects=True, vmem_limit_bytes=60 << 20
+        ),
+        name="weight_grads",
+    )(parts)
 
 
 def slot_positions(row_ids, rows_dev, peer_count, capacity):
@@ -274,16 +351,38 @@
         .at[picked_rows[1].reshape(-1)]
         .add(arrived[1].reshape(-1, table_width))
     )
-    attend_sum, output_sum, gate_sum, up_sum, down_sum, ngram_group, first_group, second_group = (
-        lax.psum_scatter(attend_grad, "dp", scatter_dimension=0, tiled=True),
-        lax.psum_scatter(output_grad, "dp", scatter_dimension=1, tiled=True),
-        lax.psum_scatter(gate_grad, "dp", scatter_dimension=0, tiled=True),
-        lax.psum_scatter(up_grad, "dp", scatter_dimension=0, tiled=True),
-        lax.psum_scatter(down_grad, "dp", scatter_dimension=1, tiled=True),
+    ngram_group, first_group, second_group = (
         lax.psum_scatter(ngram_partial, "dp", scatter_dimension=1, tiled=True),
         lax.psum_scatter(first_partial, "dp", scatter_dimension=0, tiled=True),
         lax.psum_scatter(second_partial, "dp", scatter_dimension=0, tiled=True),
     )
+    width = gate_weight.shape[0]
+    if width // peer_count % 16 == 0:
+        sides = (attend_grad.shape[1], gate_grad.shape[1], up_grad.shape[1])
+        sides += (down_grad.shape[0], output_grad.shape[0])
+        parts = jnp.concatenate(
+            [
+                item.astype(jnp.bfloat16)
+                for item in (attend_grad, gate_grad, up_grad, down_grad.T, output_grad.T)
+            ],
+            axis=1,
+        )
+        summed = reduce_over_dp(parts.reshape(peer_count, width // peer_count, -1))
+        ends = [0]
+        for side in sides:
+            ends.append(ends[-1] + side)
+        attend_sum, gate_sum, up_sum, down_sum, output_sum = (
+            summed[:, low:high] for low, high in zip(ends[:-1], ends[1:])
+        )
+        down_sum, output_sum = down_sum.T, output_sum.T
+    else:
+        attend_sum, output_sum, gate_sum, up_sum, down_sum = (
+            lax.psum_scatter(attend_grad, "dp", scatter_dimension=0, tiled=True),
+            lax.psum_scatter(output_grad, "dp", scatter_dimension=1, tiled=True),
+            lax.psum_scatter(gate_grad, "dp", scatter_dimension=0, tiled=True),
+            lax.psum_scatter(up_grad, "dp", scatter_dimension=0, tiled=True),
+            lax.psum_scatter(down_grad, "dp", scatter_dimension=1, tiled=True),
+        )
     bigram_grad, trigram_grad, ngram_grad, first_grad, second_grad = (
         lax.psum_scatter(
             bigram_part.astype(jnp.bfloat16), "tensor", scatter_dimension=0, tiled=True

time: 823 us -> 551 us (0.67)
  waiting for transfers between devices: 567 us -> 213 us
  Pallas kernels: 0 us -> 52.3 us
  matrix products: 64.9 us -> 79.1 us
  local copies, waits for them, and re-layouts: 77.9 us -> 87.1 us
    reduce_scatter x4 -> x0, waiting for transfers between devices: 273 us -> none  [the longest x1 69.7 us: shards(): lax.psum_scatter(attend_grad, 'dp', scatter_dimension=0, tiled=True)]
    unnamed x18 -> x12, waiting for transfers between devices: 65.6 us -> 11.5 us
    pallas_call x0 -> x1, Pallas kernels: none -> 52.3 us  [reduce_over_dp(): pl.pallas_call(functools.partial(reduce_kernel, peers), out_shape=jax.Sha...]
    reduce_scatter x1, waiting for transfers between devices: 24 us -> 0.01 us  [shards(): lax.psum_scatter(trigram_part.astype(jnp.bfloat16), 'tensor', scatter_dim...]
  transfers between devices with their start and end apart: 19 -> 14, of which waited for: 18 -> 11; matrix products, arithmetic and copies ran while one was open for 9% -> 15% of each run, Pallas kernels for 0% -> 10%
where the time goes in v1:
time: 551 us; the launch traced here: 545 us
  waiting for transfers between devices  213 us (39%)
  local copies, waits for them, and re-layouts  87.1 us (16%)
  matrix products  79.1 us (14%)
  other arithmetic  52.6 us (10%)
  Pallas kernels  52.3 us (9%)
  blocking collectives  24 us (4%)
  starting transfers between devices  17.8 us (3%)
  between operations  16.2 us (3%)
    pallas_call x1, Pallas kernels, reduce_over_dp(): pl.pallas_call(functools.partial(reduce_kernel, peers), out_shape=jax.Sha...  52.3 us
    reduce_scatter x1, waiting for transfers between devices, shards(): lax.psum_scatter(jnp.dot(part_rows, down_weight, preferred_element_type=j...  29.6 us
    reduce_scatter x1, waiting for transfers between devices, shards(): lax.psum_scatter(jnp.dot(part_rows, output_weight, preferred_element_type...  28.3 us
    reduce_scatter x1, waiting for transfers between devices, shards(): lax.psum_scatter((jnp.dot(gate_back, gate_weight.T, preferred_element_typ...  28.3 us
    reduce_scatter x1, waiting for transfers between devices, shards(): lax.psum_scatter(jnp.dot(part_rows, attend_weight.T, preferred_element_ty...  25.6 us
    unnamed x2, blocking collectives  24 us
    all_gather x1, waiting for transfers between devices, shards(): lax.all_gather(normed_two.astype(jnp.bfloat16), 'tensor', axis=0, tiled=T...  19.8 us
    all_gather x1, waiting for transfers between devices, shards(): lax.all_gather(after_grad.astype(jnp.bfloat16), 'tensor', axis=0, tiled=T...  19.5 us
  transfers between devices with their start and end apart: 14, of which 11 were waited for; matrix products, arithmetic and copies ran while one was open for 15% of the time, Pallas kernels for 10%

profile of v1, /device:TPU:0, one launch (start us, length us, event | category | flops | bytes accessed | tf_op | source)
XLA Modules:
  0.0 544.9 jit_solution(13054682969718759470)
XLA Ops:
  9.2 12.4 %scatter_fusion = s32[2,512]{1,0:T(2,128)S(1)} fusion(s32[2,512]{1,0:T(2,128)S(1)} %broadcast_in_dim.44, s32[256]{0:T(256)S(1)} %bitcast.161, s32[256]{0:T(256)S(1)} %get-tuple-element.377), kind=kCustom, calls=%fused_computation.4 | custom fusion | bytes 5120 | tf_op jit(solution)/shard_map/scatter | solution.py:175
  21.6 12.4 %scatter_fusion.1 = s32[2,512]{1,0:T(2,128)S(1)} fusion(s32[2,512]{1,0:T(2,128)S(1)} %scatter_fusion, s32[256]{0:T(256)S(1)} %bitcast.163, s32[256]{0:T(256)S(1)} %get-tuple-element.375), kind=kCustom, calls=%fused_computation.5 | custom fusion | bytes 5120 | tf_op jit(solution)/shard_map/scatter | solution.py:176
  34.8 7.3 %all-to-all-start = ((s32[8,1,128]{2,1,0:T(1,128)}), s32[8,1,128]{2,1,0:T(1,128)S(1)}, u32[]{:S(2)}, u32[]{:S(2)}) async-start(s32[8,1,128]{2,1,0:T(1,128)} %reshape.469), calls=%async_computation | async-start | bytes 8192 | tf_op jit(solution)/shard_map/all_to_all | solution.py:178
  59.7 13.2 %all-to-all-done.1 = bf16[2,8,64,192]{3,2,0,1:T(8,128)(2,1)S(1)} async-done(((bf16[2,8,64,192]{3,2,0,1:T(8,128)(2,1)}), bf16[2,8,64,192]{3,2,0,1:T(8,128)(2,1)S(1)}, u32[]{:S(2)}, u32[]{:S(2)}) %all-to-all-start.1) | async-done | bytes 393248 | tf_op jit(solution)/shard_map/all_to_all | solution.py:181
  78.7 18.1 %all-gather.4.cloned.1.call-done = bf16[1024,768]{1,0:T(8,128)(2,1)} async-done(((bf16[256,768]{1,0:T(8,128)(2,1)}), bf16[1024,768]{1,0:T(8,128)(2,1)}) %all-gather.4.cloned.1.call-update) | async-done | bytes 1572880 | tf_op jit(solution)/shard_map/all_gather | solution.py:188
  101.5 19.4 %while.30 = (s32[]{:T(128)}, bf16[2,512,3,64]{1,3,2,0:T(8,128)(2,1)S(1)}, f32[2,3,512]{2,1,0:T(4,128)S(1)}, s32[2]{0:T(128)S(1)}, s32[]{:T(128)}, /*index=5*/bf1...) while((s32[]{:T(128)}, ...), condition=%wide.region_8.9_spmd.clone.clone, body=%wide.region_5.8_spmd.clone.clone.sunk | while | flops 422674432 | bytes 22216900 | solution.py:223
  124.0 28.3 %reduce-scatter.11.cloned.1.call-done = bf16[256,768]{1,0:T(8,128)(2,1)} async-done(((bf16[1024,768]{1,0:T(8,128)(2,1)}), bf16[256,768]{1,0:T(8,128)(2,1)}) %reduce-scatter.11.cloned.1.call-update) | async-done | bytes 393232 | tf_op jit(solution)/shard_map/reduce_scatter | solution.py:226
  155.4 19.8 %all-gather.6.cloned.1.call-done = bf16[1024,768]{1,0:T(8,128)(2,1)} async-done(((bf16[256,768]{1,0:T(8,128)(2,1)}), bf16[1024,768]{1,0:T(8,128)(2,1)}) %all-gather.6.cloned.1.call-update) | async-done | bytes 1572880 | tf_op jit(solution)/shard_map/all_gather | solution.py:234
  185.8 28.3 %reduce-scatter.15.cloned.1.call-done = bf16[256,768]{1,0:T(8,128)(2,1)} async-done(((bf16[1024,768]{1,0:T(8,128)(2,1)}), bf16[256,768]{1,0:T(8,128)(2,1)}) %reduce-scatter.15.cloned.1.call-update) | async-done | bytes 393232 | tf_op jit(solution)/shard_map/reduce_scatter | solution.py:258
  217.8 19.5 %all-gather.8.cloned.1.call-done = bf16[1024,768]{1,0:T(8,128)(2,1)} async-done(((bf16[256,768]{1,0:T(8,128)(2,1)}), bf16[1024,768]{1,0:T(8,128)(2,1)}) %all-gather.8.cloned.1.call-update) | async-done | bytes 1572880 | tf_op jit(solution)/shard_map/all_gather | solution.py:271
  240.2 42.3 %while.31 = (s32[]{:T(128)}, f32[1024,3,64]{0,2,1:T(8,128)S(1)}, f32[1024,3,64]{0,2,1:T(8,128)}, bf16[2,512,3,64]{1,3,2,0:T(8,128)(2,1)}, s32[2]{0:T(128)S(1)}, ...) while((s32[]{:T(128)}, f32[1024,3,64]{0,2,1:T(8,128)S(1)}, ...), condition=%wide.region_16.17_spmd.clone.clone, body=%wide.region_14.16_spmd.clone.clone.sunk | while | flops 1032355840 | bytes 108319584 | solution.py:310
  291.9 25.6 %reduce-scatter.17.cloned.1.call-done = bf16[256,768]{1,0:T(8,128)(2,1)} async-done(((bf16[1024,768]{1,0:T(8,128)(2,1)}), bf16[256,768]{1,0:T(8,128)(2,1)}) %reduce-scatter.17.cloned.1.call-update) | async-done | bytes 393232 | tf_op jit(solution)/shard_map/reduce_scatter | solution.py:323
  318.8 29.6 %reduce-scatter.13.cloned.1.call-done = bf16[256,768]{1,0:T(8,128)(2,1)} async-done(((bf16[1024,768]{1,0:T(8,128)(2,1)}), bf16[256,768]{1,0:T(8,128)(2,1)}) %reduce-scatter.13.cloned.1.call-update) | async-done | bytes 393232 | tf_op jit(solution)/shard_map/reduce_scatter | solution.py:240
  353.1 13.1 %scatter_fusion.2 = f32[2,512,192]{2,1,0:T(8,128)S(1)} fusion(f32[2,512,192]{2,1,0:T(8,128)S(1)} %broadcast_in_dim.58, s32[256]{0:T(256)S(1)} %bitcast.162, f32[256,192]{1,0:T(8,128)S(1)} %get-tuple-element.362), kind=kCustom, calls=%fused_computation.6 | custom fusion | bytes 591872 | tf_op jit(solution)/shard_map/scatter | solution.py:337
  366.2 13.1 %scatter_fusion.3 = f32[2,512,192]{2,1,0:T(8,128)S(1)} fusion(f32[2,512,192]{2,1,0:T(8,128)S(1)} %scatter_fusion.2, s32[256]{0:T(256)S(1)} %bitcast.164, f32[256,192]{1,0:T(8,128)S(1)} %get-tuple-element.361), kind=kCustom, calls=%fused_computation.7 | custom fusion | bytes 591872 | tf_op jit(solution)/shard_map/scatter | solution.py:338
  380.3 5.5 %all-to-all-start.2 = ((bf16[2,8,64,192]{3,2,0,1:T(8,128)(2,1)}), bf16[2,8,64,192]{3,2,0,1:T(8,128)(2,1)S(1)}, u32[]{:S(2)}, u32[]{:S(2)}) async-start(bf16[2,8,64,192]{3,2,0,1:T(8,128)(2,1)} %copy.75), calls=%async_computation.6 | async-start | bytes 1048576 | tf_op jit(solution)/shard_map/all_to_all | solution.py:340
  386.0 14.3 %all-to-all-done.2 = bf16[2,8,64,192]{3,2,0,1:T(8,128)(2,1)S(1)} async-done(((bf16[2,8,64,192]{3,2,0,1:T(8,128)(2,1)}), bf16[2,8,64,192]{3,2,0,1:T(8,128)(2,1)S(1)}, u32[]{:S(2)}, u32[]{:S(2)}) %all-to-all-start.2) | async-done | bytes 393248 | tf_op jit(solution)/shard_map/all_to_all | solution.py:340
  400.4 5.0 scatter_custom_fusion.5
  414.2 5.0 scatter_custom_fusion.4
  431.3 5.8 %copy.76 = bf16[768,2304]{1,0:T(8,128)(2,1)} copy(bf16[768,2304]{0,1:T(8,128)(2,1)} %fusion.48) | data formatting | bytes 7077888 | tf_op jit(solution)/shard_map/concatenate | solution.py:363
  437.0 52.3 %weight_grads.1 = f32[96,2304]{1,0:T(8,128)} custom-call(bf16[8,96,2304]{2,1,0:T(8,128)(2,1)} %bitcast.165), custom_call_target="tpu_custom_call" | custom-call | tf_op jit(solution)/shard_map/weight_grads/pallas_call | solution.py:118
  495.0 18.2 %all-reduce.7 = (bf16[768]{0:T(1024)(128)(2,1)S(1)}, bf16[768]{0:T(1024)(128)(2,1)S(1)}) all-reduce(f32[768]{0:T(1024)S(1)} %get-tuple-element.291, f32[768]{0:T(1024)S(1)} %get-tuple-element.289), channel_id=10, replica_groups=mesh['dp'=8,'tensor'=4] {'dp'}, use_global_device_ids=true, to_apply=%region_28.29.clone | all-reduce | flops 1536 | bytes 9216
  513.3 5.7 %all-reduce.8 = (bf16[96]{0:T(256)(128)(2,1)S(1)}, bf16[96]{0:T(256)(128)(2,1)S(1)}) all-reduce(bf16[96]{0:T(256)(128)(2,1)S(1)} %dynamic-slice.15, bf16[96]{0:T(256)(128)(2,1)S(1)} %dynamic-slice.14), channel_id=11, replica_groups=mesh['dp'=8,'tensor'=4] {'tensor'}, use_global_device_ids=true, to_apply=%region_29.30.clone | all-reduce | flops 192 | bytes 768
  525.5 11.4 %reduce-scatter.25.cloned.1.call-done = bf16[384,24]{0,1:T(8,128)(2,1)} async-done(((bf16[384,96]{0,1:T(8,128)(2,1)}), bf16[384,24]{0,1:T(8,128)(2,1)}) %reduce-scatter.25.cloned.1.call-update) | async-done | bytes 18448
  (294 shorter events, 161.8 us)
Async XLA Ops:
  7.2 89.6 %copy-start = (bf16[768,576]{0,1:T(8,128)(2,1)S(1)}, bf16[768,576]{0,1:T(8,128)(2,1)}, u32[]{:S(2)}) copy-start(bf16[768,576]{0,1:T(8,128)(2,1)} %param.27) | copy-start | bytes 2654212
  9.1 32.9 %copy-start.31 = (bf16[2048,192]{0,1:T(8,128)(2,1)S(1)}, bf16[2048,192]{0,1:T(8,128)(2,1)}, u32[]{:S(2)}) copy-start(bf16[2048,192]{0,1:T(8,128)(2,1)} %param.23) | copy-start | bytes 2359300
  34.8 13.6 %all-to-all-start = ((s32[8,1,128]{2,1,0:T(1,128)}), s32[8,1,128]{2,1,0:T(1,128)S(1)}, u32[]{:S(2)}, u32[]{:S(2)}) async-start(s32[8,1,128]{2,1,0:T(1,128)} %reshape.469), calls=%async_computation | async-start | bytes 8192 | tf_op jit(solution)/shard_map/all_to_all | solution.py:178
  56.0 16.9 %all-to-all-start.1 = ((bf16[2,8,64,192]{3,2,0,1:T(8,128)(2,1)}), bf16[2,8,64,192]{3,2,0,1:T(8,128)(2,1)S(1)}, u32[]{:S(2)}, u32[]{:S(2)}) async-start(bf16[2,8,64,192]{3,2,0,1:T(8,128)(2,1)} %pad_maximum_fusion.1), calls=%async_computation.1 | async-start | bytes 1048576 | tf_op jit(solution)/shard_map/all_to_all | solution.py:181
  59.7 37.1 %all-gather.4.cloned.1.call-start = ((), (), s32[]{:S(2)}) async-start(), calls=%async_computation.11 | async-start | bytes 1966080 | tf_op jit(solution)/shard_map/all_gather | solution.py:188
  77.9 74.4 %reduce-scatter.11.cloned.1.call-start = ((), (), s32[]{:S(2)}) async-start(), calls=%async_computation.12 | async-start | bytes 1966080 | tf_op jit(solution)/shard_map/reduce_scatter | solution.py:226
  122.1 31.3 %copy-start.41 = (f32[768]{0:T(1024)S(1)}, f32[768]{0:T(1024)}, u32[]{:S(2)}) copy-start(f32[768]{0:T(1024)} %param.29) | copy-start | bytes 9220
  123.9 51.3 %copy-start.33 = (bf16[768,512]{1,0:T(8,128)(2,1)S(1)}, bf16[768,512]{1,0:T(8,128)(2,1)}, u32[]{:S(2)}) copy-start(bf16[768,512]{1,0:T(8,128)(2,1)} %param.30) | copy-start | bytes 2359300
  123.9 51.3 %all-gather.6.cloned.1.call-start = ((), (), s32[]{:S(2)}) async-start(), calls=%async_computation.13 | async-start | bytes 1966080 | tf_op jit(solution)/shard_map/all_gather | solution.py:234
  155.3 58.7 %reduce-scatter.15.cloned.1.call-start = ((), (), s32[]{:S(2)}) async-start(), calls=%async_computation.15 | async-start | bytes 1966080 | tf_op jit(solution)/shard_map/reduce_scatter | solution.py:258
  183.5 30.5 %copy-start.7 = (bf16[256,768]{1,0:T(8,128)(2,1)S(1)}, bf16[256,768]{1,0:T(8,128)(2,1)}, u32[]{:S(2)}) copy-start(bf16[256,768]{1,0:T(8,128)(2,1)} %reduce-scatter.11.cloned.1.call-done) | copy-start | bytes 1179652
  185.7 51.7 %all-gather.8.cloned.1.call-start = ((), (), s32[]{:S(2)}) async-start(), calls=%async_computation.16 | async-start | bytes 1966080 | tf_op jit(solution)/shard_map/all_gather | solution.py:271
  217.5 100.0 %reduce-scatter.17.cloned.1.call-start = ((), (), s32[]{:S(2)}) async-start(), calls=%async_computation.17 | async-start | bytes 1966080 | tf_op jit(solution)/shard_map/reduce_scatter | solution.py:323
  289.2 59.2 %reduce-scatter.13.cloned.1.call-start = ((), (), s32[]{:S(2)}) async-start(), calls=%async_computation.14 | async-start | bytes 1966080 | tf_op jit(solution)/shard_map/reduce_scatter | solution.py:240
  291.4 57.0 %copy-start.8 = (bf16[256,768]{1,0:T(8,128)(2,1)S(1)}, bf16[256,768]{1,0:T(8,128)(2,1)}, u32[]{:S(2)}) copy-start(bf16[256,768]{1,0:T(8,128)(2,1)} %reduce-scatter.11.cloned.1.call-done) | copy-start | bytes 1179652
  291.4 57.0 %copy-start.10 = (bf16[256,768]{1,0:T(8,128)(2,1)S(1)}, bf16[256,768]{1,0:T(8,128)(2,1)}, u32[]{:S(2)}) copy-start(bf16[256,768]{1,0:T(8,128)(2,1)} %reduce-scatter.15.cloned.1.call-done) | copy-start | bytes 1179652
  291.4 57.0 %copy-start.46 = (f32[256]{0:T(256)S(1)}, f32[256]{0:T(256)}, u32[]{:S(2)}) copy-start(f32[256]{0:T(256)} %get-tuple-element.371) | copy-start | bytes 3076
  291.4 227.7 %reduce-scatter.23.cloned.1.call-start = ((), (), s32[]{:S(2)}) async-start(), calls=%async_computation.20 | async-start | bytes 1327104 | tf_op jit(solution)/shard_map/reduce_scatter | solution.py:355
  318.8 32.1 %copy-start.25 = (bf16[256,192]{1,0:T(8,128)(2,1)S(1)}, bf16[256,192]{1,0:T(8,128)(2,1)}, u32[]{:S(2)}) copy-start(bf16[256,192]{1,0:T(8,128)(2,1)} %copy-done.24) | copy-start | bytes 294916
  318.8 32.1 %copy-start.27 = (bf16[256,192]{1,0:T(8,128)(2,1)S(1)}, bf16[256,192]{1,0:T(8,128)(2,1)}, u32[]{:S(2)}) copy-start(bf16[256,192]{1,0:T(8,128)(2,1)} %copy-done.26) | copy-start | bytes 294916
  380.3 20.0 %all-to-all-start.2 = ((bf16[2,8,64,192]{3,2,0,1:T(8,128)(2,1)}), bf16[2,8,64,192]{3,2,0,1:T(8,128)(2,1)S(1)}, u32[]{:S(2)}, u32[]{:S(2)}) async-start(bf16[2,8,64,192]{3,2,0,1:T(8,128)(2,1)} %copy.75), calls=%async_computation.6 | async-start | bytes 1048576 | tf_op jit(solution)/shard_map/all_to_all | solution.py:340
  385.8 136.0 %reduce-scatter.21.cloned.1.call-start = ((), (), s32[]{:S(2)}) async-start(), calls=%async_computation.19 | async-start | bytes 1310720 | tf_op jit(solution)/shard_map/reduce_scatter | solution.py:390
  408.2 115.5 %reduce-scatter.19.cloned.1.call-start = ((), (), s32[]{:S(2)}) async-start(), calls=%async_computation.18 | async-start | bytes 1310720 | tf_op jit(solution)/shard_map/reduce_scatter | solution.py:387
  421.9 114.9 %reduce-scatter.25.cloned.1.call-start = ((), (), s32[]{:S(2)}) async-start(), calls=%async_computation.21 | async-start | bytes 92160
  (49 other events, 373.0 us)
Sparse Core Ops, SparseCore 0:
  78.0 18.7 all-gather.3
  124.0 28.1 reduce-scatter.10
  155.5 19.6 all-gather.5
  185.8 28.1 reduce-scatter.14
  217.7 19.6 all-gather.7
  289.3 28.1 reduce-scatter.16
  320.2 28.1 reduce-scatter.12
  352.5 64.2 reduce-scatter.22
  419.4 23.8 reduce-scatter.20
  445.8 24.8 reduce-scatter.18
  520.8 16.0 reduce-scatter.24

commit v2 on v0

v2 whole, which is shorter than its diff:
```python
import functools
import math

import jax
import jax.numpy as jnp
from jax import lax
from jax.experimental import pallas as pl
from jax.experimental.pallas import tpu as pltpu
from jax.sharding import PartitionSpec as P

BF = jnp.bfloat16
F32 = jnp.float32
HD = 64
LANES = 128
PREFIX_MOST = 512
SPLIT = 4
CHUNKS = 4

INPUTS = (
    "embedded", "bigram_ids", "trigram_ids", "prefix", "bigram_table", "trigram_table",
    "ngram_weight", "first_gain", "attend_weight", "output_weight", "second_gain",
    "gate_weight", "up_weight", "down_weight", "cotangent",
)


class Refs:
    def __init__(self, names, refs):
        self.__dict__.update(zip(names, refs, strict=True))


def dot(left, right):
    return jnp.dot(left, right, preferred_element_type=F32)


def dot_right(left, right):
    return lax.dot_general(left, right, (((1,), (1,)), ((), ())), preferred_element_type=F32)


def lane_of(shape):
    return lax.broadcasted_iota(jnp.int32, shape, len(shape) - 1)


def row_of(shape):
    return lax.broadcasted_iota(jnp.int32, shape, 0)


def onehot(test):
    return jnp.where(test, 1.0, 0.0).astype(BF)


def roll64(block):
    return pltpu.roll(block, 64, 1)


def swap_halves(block):
    return jnp.where(lane_of(block.shape) < 32, pltpu.roll(block, 96, 1), pltpu.roll(block, 32, 1))


class Sizes:
    def __init__(self, n, rows, width, heads, units, table_rows, table_width):
        self.n, self.rows, self.width, self.heads, self.units = n, rows, width, heads, units
        self.table_rows, self.table_width = table_rows, table_width
        self.length = rows * SPLIT
        self.keys = [max((i + 1) * rows, min(PREFIX_MOST, rows * SPLIT)) for i in range(SPLIT)]
        self.cap = max(16, 2 * rows // n)
        self.slots = n * self.cap
        self.padded = heads * LANES
        self.chunk = rows // CHUNKS
        self.piece = width // n
        self.groups = n // 2
        self.pair_width = 2 * table_width
        self.small = width // (n * SPLIT)
        self.small_lanes = self.pair_width + LANES
        self.attn_lanes = heads * HD * 4
        self.inside = self.piece % 16 == 0 and self.small % 8 == 0


def make_copy(src, dst, send, recv, **where):
    return pltpu.make_async_remote_copy(
        src_ref=src, dst_ref=dst, send_sem=send, recv_sem=recv, device_id=where
    )


class Gather:
    def __init__(self, z, pos, full, sems):
        self.z, self.pos, self.full, self.sems = z, pos, full, sems

    def piece(self, block, c):
        start = pl.multiple_of(block * self.z.rows + c * self.z.chunk, self.z.chunk)
        return self.full.at[pl.ds(start, self.z.chunk)]

    def copy(self, kind, c, incoming=False):
        p = self.pos
        block = ((p.t, p.t1), (p.t, p.t2), (p.t2, p.t3))[kind][1 if incoming else 0]
        ref = self.piece(block, c)
        target = p.t2 if kind == 1 else p.t1
        return make_copy(
            ref, ref, self.sems.at[c, 2 * kind], self.sems.at[c, 2 * kind + 1], tensor=target
        )

    def send(self, c):
        self.copy(1, c).start()
        self.copy(0, c).start()

    def receive(self, c):
        self.copy(1, c, True).wait_recv()
        self.copy(2, c).start()
        self.copy(0, c, True).wait_recv()
        self.copy(2, c, True).wait_recv()

    def close(self):
        def body(c, carry):
            for kind in range(3):
                self.copy(kind, c).wait_send()
            return carry

        lax.fori_loop(0, CHUNKS, body, 0)


class Scatter:
    def __init__(self, z, pos, part, near, out, far, sems):
        self.z, self.pos, self.part, self.near = z, pos, part, near
        self.out, self.far, self.sems = out, far, sems

    def span(self, c):
        return pl.ds(pl.multiple_of(c * self.z.chunk, self.z.chunk), self.z.chunk)

    def rows(self, block, c):
        start = pl.multiple_of(block * self.z.rows + c * self.z.chunk, self.z.chunk)
        return pl.ds(start, self.z.chunk)

    def near_copy(self, slot, c):
        block = self.pos.t3 if slot else self.pos.t1
        return make_copy(
            self.part.at[self.rows(block, c)],
            self.near.at[slot, self.span(c)],
            self.sems.at[c, 2 * slot],
            self.sems.at[c, 2 * slot + 1],
            tensor=self.pos.t1,
        )

    def far_copy(self, c):
        return make_copy(
            self.out.at[self.span(c)],
            self.far.at[self.span(c)],
            self.sems.at[c, 4],
            self.sems.at[c, 5],
            tensor=self.pos.t2,
        )

    def send(self, c):
        self.near_copy(1, c).start()
        self.near_copy(0, c).start()

    def middle(self, c):
        self.near_copy(1, c).wait_recv()
        own = self.part[self.rows(self.pos.t2, c)].astype(F32)
        self.out[self.span(c)] = (own + self.near[1, self.span(c)].astype(F32)).astype(BF)
        self.far_copy(c).start()

    def finish(self, c):
        self.near_copy(0, c).wait_recv()
        self.far_copy(c).wait_recv()
        own = self.part[self.rows(self.pos.t, c)].astype(F32)
        own = own + self.near[0, self.span(c)].astype(F32)
        return own + self.far[self.span(c)].astype(F32)

    def close(self):
        def body(c, carry):
            self.near_copy(0, c).wait_send()
            self.near_copy(1, c).wait_send()
            self.far_copy(c).wait_send()
            return carry

        lax.fori_loop(0, CHUNKS, body, 0)


class Spread:
    def __init__(self, z, pos, part, pair_in, pair_out, far_in, out, sems):
        self.z, self.pos, self.part, self.pair_in = z, pos, part, pair_in
        self.pair_out, self.far_in, self.out, self.sems = pair_out, far_in, out, sems

    def group(self, step):
        return lax.rem(self.pos.place + step, self.z.groups)

    def rows(self, peer):
        return pl.ds(pl.multiple_of(peer * self.z.piece, self.z.piece), self.z.piece)

    def near_copy(self, step):
        group = self.group(step)
        return make_copy(
            self.part.at[self.rows(group * 2 + 1 - self.pos.parity)],
            self.pair_in.at[step - 1],
            self.sems.at[0, step - 1],
            self.sems.at[1, step - 1],
            dp=self.pos.partner,
        )

    def far_copy(self, step):
        return make_copy(
            self.pair_out.at[step - 1],
            self.far_in.at[step - 1],
            self.sems.at[2, step - 1],
            self.sems.at[3, step - 1],
            dp=self.group(step) * 2 + self.pos.parity,
        )

    def send(self):
        for step in range(1, self.z.groups + 1):
            self.near_copy(step).start()

    def middle(self, step):
        self.near_copy(step).wait_recv()
        own = self.part[self.rows(self.group(step) * 2 + self.pos.parity)].astype(F32)
        total = own + self.pair_in[step - 1].astype(F32)
        if step == self.z.groups:
            self.out[...] = total
        else:
            self.pair_out[step - 1] = total.astype(BF)
            self.far_copy(step).start()

    def finish(self):
        for step in range(1, self.z.groups):
            self.far_copy(step).wait_recv()
            self.out[...] += self.far_in[step - 1].astype(F32)

    def close(self):
        for step in range(1, self.z.groups + 1):
            self.near_copy(step).wait_send()
            if step < self.z.groups:
                self.far_copy(step).wait_send()


class Position:
    def __init__(self, z):
        self.d, self.t = lax.axis_index("dp"), lax.axis_index("tensor")
        core, side = lax.rem(self.t, 2), self.t // 2
        self.t1 = self.t + 1 - 2 * core
        self.t2 = self.t + 2 - 4 * side
        self.t3 = self.t1 + 2 - 4 * side
        self.parity, self.place = lax.rem(self.d, 2), self.d // 2
        self.partner = self.d + 1 - 2 * self.parity


def scratch_of(z):
    n, rows, width, length, chunks = z.n, z.rows, z.width, z.length, CHUNKS
    vmem, dma = pltpu.VMEM, pltpu.SemaphoreType.DMA
    shapes = dict(
        emb=vmem((rows, width), BF),
        ids=vmem((2 * n, 1, rows), jnp.int32),
        own_ids=vmem((2, 1, rows), jnp.int32),
        table_b=vmem((z.table_rows, z.table_width), BF),
        table_t=vmem((z.table_rows, z.table_width), BF),
        nw=vmem((z.pair_width, width), BF),
        gain1=vmem((1, width), F32),
        gain2=vmem((1, width), F32),
        wa=vmem((width, 3 * z.heads * HD), BF),
        wap=vmem((width, 3 * z.padded), BF),
        wo=vmem((z.heads * HD, width), BF),
        wop=vmem((z.padded, width), BF),
        wgu=vmem((width, 2 * z.units), BF),
        wd=vmem((z.units, width), BF),
        cot=vmem((length, width), BF),
        cosine=vmem((length, LANES), F32),
        sines=vmem((length, LANES), F32),
        pick=vmem((2, rows, z.slots), BF),
        pick_t=vmem((2, z.slots, rows), BF),
        lids=vmem((SPLIT, 2, 8, z.slots), jnp.int32),
        rows_out=vmem((z.slots, z.pair_width), BF),
        rows_in=vmem((z.slots, z.pair_width), BF),
        grams=vmem((rows, z.pair_width), BF),
        inputs=vmem((rows, width), F32),
        after=vmem((rows, width), F32),
        aftergrad=vmem((rows, width), F32),
        scale1=vmem((rows, LANES), F32),
        scale2=vmem((rows, LANES), F32),
        n1=vmem((length, width), BF),
        n2=vmem((length, width), BF),
        ab=vmem((length, width), BF),
        q=vmem((length, z.padded), BF),
        k=vmem((length, z.padded), BF),
        v=vmem((length, z.padded), BF),
        probs0=vmem((z.heads, rows, z.keys[0]), BF),
        probs1=vmem((z.heads, rows, z.keys[1]), BF),
        probs2=vmem((z.heads, rows, z.keys[2]), BF),
        probs3=vmem((z.heads, rows, z.keys[3]), BF),
        att=vmem((length, z.padded), BF),
        do=vmem((length, z.padded), BF),
        dk=vmem((z.heads, HD, length), F32),
        dv=vmem((z.heads, HD, length), F32),
        mixb=vmem((length, 3 * z.padded), BF),
        act=vmem((length, z.units), BF),
        gub=vmem((length, 2 * z.units), BF),
        lifted=vmem((rows, width), BF),
        sums=vmem((2, 8, width), F32),
        back_out=vmem((z.slots, z.pair_width), BF),
        back_in=vmem((SPLIT * z.slots, z.pair_width), BF),
        in_sem=dma((16,)),
        id_sem=dma((2,)),
        row_sem=dma((2, n)),
        lid_sem=dma((2, 3)),
        back_sem=dma((2, n)),
        pass_sem=dma((6, n)),
        ag1_sem=dma((chunks, 6)),
        ag2_sem=dma((chunks, 6)),
        ag3_sem=dma((chunks, 6)),
    )
    for k in range(1, 4):
        shapes[f"part{k}"] = vmem((length, width), BF)
        shapes[f"near{k}"] = vmem((2, rows, width), BF)
        shapes[f"send{k}"] = vmem((rows, width), BF)
        shapes[f"far{k}"] = vmem((rows, width), BF)
        shapes[f"rs{k}_sem"] = dma((chunks, 6))
    shapes["rs4_sem"] = dma((chunks, 6))
    if z.inside:
        for name, lanes in (("gu", 2 * z.units), ("dn", z.units), ("at", z.attn_lanes)):
            shapes[f"{name}_part"] = vmem((width, lanes), BF)
            shapes[f"{name}_pair_in"] = vmem((z.groups, z.piece, lanes), BF)
            shapes[f"{name}_pair_out"] = vmem((z.groups - 1, z.piece, lanes), BF)
            shapes[f"{name}_far_in"] = vmem((z.groups - 1, z.piece, lanes), BF)
            shapes[f"{name}_sem"] = dma((4, z.groups))
        small = (n, z.small, z.small_lanes)
        shapes["sm_part"] = vmem((SPLIT, *small), BF)
        shapes["sm_near"] = vmem((2, *small), BF)
        shapes["sm_send"] = vmem(small, BF)
        shapes["sm_far"] = vmem(small, BF)
        shapes["sm_out"] = vmem(small, BF)
        shapes["sm_in"] = vmem(small, BF)
        shapes["sm_sem"] = dma((6,))
        shapes["sp_sem"] = dma((2, n))
    return shapes


def outputs_of(z):
    n, rows, width = z.n, z.rows, z.width
    shapes = dict(
        block_out=((rows, width), BF),
        embed_grad=((rows, width), F32),
        table_grads=((z.table_rows // SPLIT, z.pair_width), F32),
    )
    if z.inside:
        shapes["gu_out"] = ((z.piece, 2 * z.units), F32)
        shapes["dn_out"] = ((z.piece, z.units), F32)
        shapes["at_out"] = ((z.piece, z.attn_lanes), F32)
        shapes["sm_total"] = ((z.small, z.small_lanes), F32)
    else:
        shapes["gu_part"] = ((width, 2 * z.units), BF)
        shapes["dn_part"] = ((width, z.units), BF)
        shapes["at_part"] = ((width, z.attn_lanes), BF)
        shapes["sm_total"] = ((width, z.small_lanes), F32)
    return shapes


def block_kernel(z, names, *refs):
    r = Refs(names, refs)
    p = Position(z)
    n, rows, width, length = z.n, z.rows, z.width, z.length
    cap, slots, units, padded, heads = z.cap, z.slots, z.units, z.padded, z.heads
    gather1 = Gather(z, p, r.n1, r.ag1_sem)
    gather2 = Gather(z, p, r.n2, r.ag2_sem)
    gather3 = Gather(z, p, r.ab, r.ag3_sem)
    scatters = [
        Scatter(
            z, p, getattr(r, f"part{k}"), getattr(r, f"near{k}"), getattr(r, f"send{k}"),
            getattr(r, f"far{k}"), sems,
        )
        for k, sems in ((1, r.rs1_sem), (2, r.rs2_sem), (3, r.rs3_sem), (1, r.rs4_sem))
    ]
    scatter1, scatter2, scatter3, scatter4 = scatters
    spreads = {}
    if z.inside:
        for name in ("gu", "dn", "at"):
            spreads[name] = Spread(
                z, p, getattr(r, f"{name}_part"), getattr(r, f"{name}_pair_in"),
                getattr(r, f"{name}_pair_out"), getattr(r, f"{name}_far_in"),
                getattr(r, f"{name}_out"), getattr(r, f"{name}_sem"),
            )

    def peer(step):
        return lax.rem(p.d + step, n)

    barrier = pltpu.get_barrier_semaphore()
    for step in range(1, n):
        pl.semaphore_signal(barrier, inc=1, device_id={"dp": peer(step)})
    for target in (p.t1, p.t2, p.t3):
        pl.semaphore_signal(barrier, inc=1, device_id={"tensor": target})

    loads = [
        (r.bigram_ids, r.own_ids.at[0]),
        (r.trigram_ids, r.own_ids.at[1]),
        (r.bigram_table, r.table_b),
        (r.trigram_table, r.table_t),
        (r.attend_weight, r.wa),
        (r.output_weight, r.wo),
        (r.embedded, r.emb),
        (r.ngram_weight, r.nw),
        (r.first_gain, r.gain1),
        (r.second_gain, r.gain2),
        (r.gate_weight, r.wgu.at[:, pl.ds(0, units)]),
        (r.up_weight, r.wgu.at[:, pl.ds(units, units)]),
        (r.down_weight, r.wd),
        (r.cotangent, r.cot),
    ]
    loads = [pltpu.make_async_copy(src, dst, r.in_sem.at[i]) for i, (src, dst) in enumerate(loads)]
    for load in loads:
        load.start()

    pl.semaphore_wait(barrier, n - 1 + 3)

    def id_copy(step, k):
        return make_copy(
            (r.bigram_ids, r.trigram_ids)[k],
            r.ids.at[k * n + p.d],
            r.id_sem.at[0],
            r.id_sem.at[1],
            dp=peer(step),
        )

    for step in range(1, n):
        for k in range(2):
            id_copy(step, k).start()

    lane = lane_of((32, LANES))
    low = jnp.where(lane < 32, lane, lane - 32)
    frequency = jnp.exp(low.astype(F32) * (-2.0 * math.log(10000.0) / HD))
    place = row_of((32, LANES)).astype(F32)
    coarse, fine = place * 32.0 * frequency, place * frequency
    cos_coarse, sin_coarse = jnp.cos(coarse), jnp.sin(coarse)
    used = lane < HD
    cos_fine = jnp.where(used, jnp.cos(fine), 0.0)
    sin_fine = jnp.where(used, jnp.sin(fine), 0.0)
    sign = jnp.where(lane < 32, -1.0, 1.0)
    for a in range(length // 32):
        ca, sa = cos_coarse[a : a + 1], sin_coarse[a : a + 1]
        r.cosine[a * 32 : (a + 1) * 32] = ca * cos_fine - sa * sin_fine
        r.sines[a * 32 : (a + 1) * 32] = sign * (sa * cos_fine + ca * sin_fine)

    loads[0].wait()
    loads[1].wait()
    earlier = onehot(row_of((rows, rows)) < lane_of((rows, rows)))
    later = onehot(row_of((rows, rows)) > lane_of((rows, rows)))
    for k in range(2):
        r.ids[k * n + p.d] = r.own_ids[k]
        own = jnp.broadcast_to(r.own_ids[k].astype(F32), (LANES, rows))
        column = own.T
        start = (lane_of((rows, LANES)) * z.table_rows).astype(F32)
        held = (column >= start) & (column < start + z.table_rows)
        ranks = dot(later, onehot(held))
        slot = jnp.where(held, ranks + (lane_of((rows, LANES)) * cap).astype(F32), 0.0)
        slot = jnp.sum(slot, axis=1, keepdims=True)
        r.pick[k] = onehot(slot.astype(jnp.int32) == lane_of((rows, slots)))
        across = jnp.broadcast_to(slot, (rows, LANES)).T[0:1]
        r.pick_t[k] = onehot(across.astype(jnp.int32) == row_of((slots, rows)))

    loads[4].wait()
    low_half = lane_of((width, LANES)) < HD
    for h in range(heads):
        for c in range(3):
            at = (3 * h + c) * HD
            block = r.wa[:, at // LANES * LANES : min(at // LANES * LANES + LANES, 3 * heads * HD)]
            block = block.astype(F32)
            if block.shape[1] < LANES:
                fill = jnp.zeros((width, LANES - block.shape[1]), F32)
                block = jnp.concatenate([block, fill], axis=1)
            if at % LANES:
                block = roll64(block)
            to = c * padded + h * LANES
            r.wap[:, to : to + LANES] = jnp.where(low_half, block, 0.0).astype(BF)
    loads[5].wait()
    for h in range(heads):
        r.wop[h * LANES : h * LANES + HD] = r.wo[h * HD : (h + 1) * HD]
        r.wop[h * LANES + HD : (h + 1) * LANES] = jnp.zeros((HD, width), BF)

    loads[2].wait()
    loads[3].wait()
    all_ids = r.ids.at[pl.ds(0, 2 * (n - 1))]
    all_ids = make_copy(all_ids, all_ids, r.id_sem.at[0], r.id_sem.at[1], dp=peer(1))
    all_ids.wait_recv()
    asked = jnp.concatenate([r.ids[i] for i in range(2 * n)], axis=0)
    first_row = p.d * z.table_rows
    mine = (asked >= first_row) & (asked < first_row + z.table_rows)
    ranks = dot(onehot(mine), earlier)
    tags = jnp.where(mine, ranks, -1.0).astype(jnp.int32)
    local = jnp.where(mine, asked - first_row + 1, 0).astype(F32)
    picked = []
    for k in range(2):
        columns = []
        for i in range(n):
            at = k * n + i
            hit = tags[at : at + 1] == row_of((cap, rows))
            value = jnp.where(hit, local[at : at + 1], 0.0)
            columns.append(jnp.sum(value, axis=1, keepdims=True) - 1.0)
        column = jnp.concatenate(columns, axis=0)
        picked.append(column.astype(jnp.int32))
        across = jnp.broadcast_to(column, (slots, LANES)).T[0:8]
        r.lids[p.t, k] = across.astype(jnp.int32)
    half = slots // 2

    def row_copy(step):
        to = peer(step)
        return make_copy(
            r.rows_out.at[pl.ds(pl.multiple_of(to * cap, cap), cap)],
            r.rows_in.at[pl.ds(pl.multiple_of(p.d * cap, cap), cap)],
            r.row_sem.at[0, 0],
            r.row_sem.at[1, p.d],
            dp=to,
        )

    def row_arrival(step):
        of = peer(step)
        ref = r.rows_in.at[pl.ds(pl.multiple_of(of * cap, cap), cap)]
        return make_copy(ref, ref, r.row_sem.at[0, 0], r.row_sem.at[1, of], dp=of)

    for part in range(2):
        found = []
        for k, table in enumerate((r.table_b, r.table_t)):
            chosen = picked[k][part * half : (part + 1) * half]
            hits = onehot(chosen == lane_of((half, z.table_rows)))
            both = dot(hits, table[...])
            fill = jnp.zeros((half, 2 * LANES - z.table_width), F32)
            found.append((both[:, :LANES], jnp.concatenate([both[:, LANES:], fill], axis=1)))
        low_half = lane_of((half, LANES)) < HD
        rolled = [roll64(block) for block in found[1]]
        span = slice(part * half, (part + 1) * half)
        r.rows_out[span, 0:LANES] = found[0][0].astype(BF)
        middle = jnp.where(low_half, found[0][1], rolled[0])
        r.rows_out[span, LANES : 2 * LANES] = middle.astype(BF)
        r.rows_out[span, 2 * LANES :] = jnp.where(low_half, rolled[0], rolled[1]).astype(BF)
    for step in range(1, n):
        row_copy(n - step).start()
    own_slots = pl.ds(pl.multiple_of(p.d * cap, cap), cap)
    r.rows_in[own_slots] = r.rows_out[own_slots]

    for load in loads[6:10]:
        load.wait()
    for step in range(1, n):
        row_arrival(step).wait_recv()
    fetched = r.rows_in[...]
    low_table = lane_of((rows, z.pair_width)) < z.table_width
    grams = jnp.where(low_table, dot(r.pick[0], fetched), dot(r.pick[1], fetched)).astype(BF)
    r.grams[...] = grams
    inputs = r.emb[...].astype(F32) + dot(grams, r.nw[...])
    r.inputs[...] = inputs
    scale = lax.rsqrt(jnp.mean(inputs * inputs, axis=1, keepdims=True) + 1e-05)
    r.scale1[...] = jnp.broadcast_to(scale, (rows, LANES))
    own_rows = pl.ds(pl.multiple_of(p.t * rows, rows), rows)
    r.n1[own_rows] = (inputs * scale * r.gain1[...]).astype(BF)
    for c in range(CHUNKS):
        gather1.send(c)

    def lid_copy(i, incoming=False):
        target = (p.t1, p.t2, p.t3)[i]
        ref = r.lids.at[target if incoming else p.t]
        return make_copy(ref, ref, r.lid_sem.at[0, i], r.lid_sem.at[1, i], tensor=target)

    for i in range(3):
        lid_copy(i).start()

    def spans(c):
        return [
            pl.ds(pl.multiple_of(b * rows + c * z.chunk, z.chunk), z.chunk) for b in range(SPLIT)
        ]

    def take(ref, c, *rest):
        return jnp.concatenate([ref[(span, *rest)] for span in spans(c)], axis=0)

    def put(ref, c, value, *rest):
        for b, span in enumerate(spans(c)):
            ref[(span, *rest)] = value[b * z.chunk : (b + 1) * z.chunk]

    def project(c, carry):
        gather1.receive(c)
        mixture = dot(take(r.n1, c), r.wap[...])
        cosine, sines = take(r.cosine, c), take(r.sines, c)
        for h in range(heads):
            for i, (ref, factor) in enumerate(((r.q, HD**-0.5), (r.k, 1.0))):
                at = i * padded + h * LANES
                block = mixture[:, at : at + LANES]
                turned = (block * cosine + swap_halves(block) * sines).astype(BF)
                if factor != 1.0:
                    turned = (turned.astype(F32) * factor).astype(BF)
                put(ref, c, turned, slice(h * LANES, (h + 1) * LANES))
        put(r.v, c, mixture[:, 2 * padded :].astype(BF))
        return carry

    lax.fori_loop(0, CHUNKS, project, 0)

    prefix = r.prefix[0]
    probs = (r.probs0, r.probs1, r.probs2, r.probs3)
    blocks = [(i * rows, z.keys[i], probs[i]) for i in range(SPLIT)]

    def head_lanes(h):
        return pl.ds(pl.multiple_of(h * LANES, LANES), LANES)

    def attend(first, keys, kept):
        span = slice(first, first + rows)

        def one_head(h, carry):
            at = head_lanes(h)
            scores = dot_right(r.q[span, at], r.k[0:keys, at])
            key = lane_of((rows, keys))
            allowed = (key <= row_of((rows, keys)) + first) | (key < prefix)
            scores = jnp.where(allowed, scores, -1000000000.0)
            powers = jnp.exp(scores - jnp.max(scores, axis=1, keepdims=True))
            inverse = 1.0 / jnp.sum(powers, axis=1, keepdims=True)
            weights = (powers * inverse).astype(BF)
            kept[h] = weights
            r.att[span, at] = dot(weights, r.v[0:keys, at]).astype(BF)
            return carry

        lax.fori_loop(0, heads, one_head, 0)
        r.part1[span] = dot(r.att[span], r.wop[...]).astype(BF)

    for block in blocks:
        attend(*block)
    for c in range(CHUNKS):
        scatter1.send(c)
    for c in range(CHUNKS):
        scatter1.middle(c)

    for load in loads[10:]:
        load.wait()

    def second_norm(c, carry):
        span = scatter1.span(c)
        after = r.inputs[span] + scatter1.finish(c)
        r.after[span] = after
        scale = lax.rsqrt(jnp.mean(after * after, axis=1, keepdims=True) + 1e-05)
        r.scale2[span] = jnp.broadcast_to(scale, (z.chunk, LANES))
        own = scatter1.rows(p.t, c)
        r.n2[own] = (after * scale * r.gain2[...]).astype(BF)
        gather2.send(c)
        return carry

    lax.fori_loop(0, CHUNKS, second_norm, 0)

    def feed_forward(c, carry):
        gather2.receive(c)
        both = dot(take(r.n2, c), r.wgu[...])
        act_back = dot_right(take(r.cot, c), r.wd[...])
        gate, up = both[:, :units], both[:, units:]
        s = 1.0 / (1.0 + jnp.exp(-gate))
        silu = gate * s
        put(r.act, c, (silu * up).astype(BF))
        gate_back = (act_back * up * s * (1.0 + gate * (1.0 - s))).astype(BF)
        up_back = (act_back * silu).astype(BF)
        put(r.gub, c, gate_back, slice(0, units))
        put(r.gub, c, up_back, slice(units, 2 * units))
        back = dot_right(gate_back, r.wgu[:, 0:units]) + dot_right(up_back, r.wgu[:, units:])
        put(r.part3, c, back.astype(BF))
        scatter3.send(c)
        return carry

    lax.fori_loop(0, CHUNKS, feed_forward, 0)
    for c in range(CHUNKS):
        scatter3.middle(c)

    tile = 2 * LANES

    def gate_up_tile(j, carry):
        at = pl.ds(pl.multiple_of(j * tile, tile), tile)
        r.gu_part[at] = dot(r.n2[:, at].T, r.gub[...]).astype(BF)
        return carry

    lax.fori_loop(0, width // tile, gate_up_tile, 0)
    if z.inside:
        spreads["gu"].send()

    r.sums[...] = jnp.zeros_like(r.sums)

    def norm_back(grad, values, scale, gain):
        scaled = grad * gain
        mean = jnp.mean(scaled * values, axis=1, keepdims=True)
        total = jnp.sum(grad * values * scale, axis=0, keepdims=True)
        return scale * scaled - values * (scale * scale * scale * mean), total

    def second_back(c, carry):
        span = scatter3.span(c)
        grad = scatter3.finish(c)
        row_grad, total = norm_back(grad, r.after[span], r.scale2[span, 0:1], r.gain2[...])
        r.sums[1, 0:1] += total
        own = scatter3.rows(p.t, c)
        after_grad = r.cot[own].astype(F32) + row_grad
        r.aftergrad[span] = after_grad
        r.ab[own] = after_grad.astype(BF)
        gather3.send(c)
        return carry

    lax.fori_loop(0, CHUNKS, second_back, 0)

    def branch_two(c, carry):
        put(r.part2, c, dot(take(r.act, c), r.wd[...]).astype(BF))
        scatter2.send(c)
        return carry

    lax.fori_loop(0, CHUNKS, branch_two, 0)
    for c in range(CHUNKS):
        scatter2.middle(c)

    def down_tile(j, carry):
        at = pl.ds(pl.multiple_of(j * tile, tile), tile)
        r.dn_part[at] = dot(r.cot[:, at].T, r.act[...]).astype(BF)
        return carry

    lax.fori_loop(0, width // tile, down_tile, 0)
    if z.inside:
        spreads["dn"].send()

    def attended_back(c, carry):
        gather3.receive(c)
        put(r.do, c, dot_right(take(r.ab, c), r.wop[...]).astype(BF))
        return carry

    lax.fori_loop(0, CHUNKS, attended_back, 0)
    r.dk[...] = jnp.zeros_like(r.dk)
    r.dv[...] = jnp.zeros_like(r.dv)

    def unrotate(grads, span):
        grads = grads.astype(BF).astype(F32)
        turned = grads * r.cosine[span] - swap_halves(grads) * r.sines[span]
        return turned.astype(BF)

    def attend_back(first, keys, kept):
        span = slice(first, first + rows)

        def one_head(h, carry):
            at = head_lanes(h)
            do, q = r.do[span, at], r.q[span, at]
            weights = kept[h]
            prob_back = dot_right(do, r.v[0:keys, at])
            centre = jnp.sum(do.astype(F32) * r.att[span, at].astype(F32), axis=1, keepdims=True)
            score_back = (weights.astype(F32) * (prob_back - centre)).astype(BF)
            query_back = dot(score_back, r.k[0:keys, at]) * HD**-0.5
            r.mixb[span, at] = unrotate(query_back, span)
            r.dk[h, :, 0:keys] += dot(q.T[:HD], score_back)
            r.dv[h, :, 0:keys] += dot(do.T[:HD], weights)
            return carry

        lax.fori_loop(0, heads, one_head, 0)

    for block in blocks:
        attend_back(*block)

    def block_out(c, carry):
        span = scatter2.span(c)
        r.block_out[span] = (r.after[span] + scatter2.finish(c)).astype(BF)
        return carry

    lax.fori_loop(0, CHUNKS, block_out, 0)

    def upright(block):
        return jnp.concatenate([block, jnp.zeros_like(block)], axis=0).T

    scatter1.close()
    for h in range(heads):
        for i in range(SPLIT):
            span = slice(i * rows, (i + 1) * rows)
            at = padded + h * LANES
            r.mixb[span, at : at + LANES] = unrotate(upright(r.dk[h, :, span]), span)
            at = 2 * padded + h * LANES
            r.mixb[span, at : at + LANES] = upright(r.dv[h, :, span]).astype(BF)

    def first_norm_part(c, carry):
        put(r.part1, c, dot_right(take(r.mixb, c), r.wap[...]).astype(BF))
        scatter4.send(c)
        return carry

    lax.fori_loop(0, CHUNKS, first_norm_part, 0)
    for c in range(CHUNKS):
        scatter4.middle(c)
    if z.inside:
        for step in range(1, z.groups + 1):
            spreads["gu"].middle(step)

    def attend_tile(j, carry):
        at = pl.ds(pl.multiple_of(j * tile, tile), tile)
        grad = dot(r.n1[:, at].T, r.mixb[...])
        outer = dot(r.ab[:, at].T, r.att[...])
        parts = []
        for h in range(heads):
            for c in range(3):
                start = c * padded + h * LANES
                parts.append(grad[:, start : start + LANES])
        for h in range(heads):
            parts.append(outer[:, h * LANES : (h + 1) * LANES])
        for g in range(len(parts) // 2):
            both = parts[2 * g] + roll64(parts[2 * g + 1])
            r.at_part[at, g * LANES : (g + 1) * LANES] = both.astype(BF)
        return carry

    lax.fori_loop(0, width // tile, attend_tile, 0)
    if z.inside:
        spreads["at"].send()

    def first_back(c, carry):
        span = scatter4.span(c)
        grad = scatter4.finish(c)
        row_grad, total = norm_back(grad, r.inputs[span], r.scale1[span, 0:1], r.gain1[...])
        r.sums[0, 0:1] += total
        embed_grad = r.aftergrad[span] + row_grad
        r.embed_grad[span] = embed_grad
        r.lifted[span] = embed_grad.astype(BF)
        return carry

    lax.fori_loop(0, CHUNKS, first_back, 0)

    row_back = dot_right(r.lifted[...], r.nw[...]).astype(BF)
    low_table = lane_of((slots, z.pair_width)) < z.table_width
    outgoing = jnp.where(low_table, dot(r.pick_t[0], row_back), dot(r.pick_t[1], row_back))
    r.back_out[...] = outgoing.astype(BF)

    def back_slots(block, of):
        return r.back_in.at[pl.ds(pl.multiple_of(block * slots + of * cap, cap), cap)]

    def back_copy(step, incoming=False):
        to = peer(step)
        src = r.back_out.at[pl.ds(pl.multiple_of(to * cap, cap), cap)]
        dst = back_slots(p.t, to if incoming else p.d)
        recv = r.back_sem.at[1, to if incoming else p.d]
        return make_copy(src, dst, r.back_sem.at[0, 0], recv, dp=to)

    def pass_copy(kind, of, incoming=False):
        block = ((p.t, p.t1), (p.t, p.t2), (p.t2, p.t3))[kind][1 if incoming else 0]
        ref = back_slots(block, of)
        target = p.t2 if kind == 1 else p.t1
        return make_copy(
            ref, ref, r.pass_sem.at[2 * kind, of], r.pass_sem.at[2 * kind + 1, of], tensor=target
        )

    for step in range(1, n):
        back_copy(n - step).start()
    own_block = pl.ds(pl.multiple_of(p.t * slots + p.d * cap, cap), cap)
    r.back_in[own_block] = r.back_out[own_slots]

    gains = jnp.concatenate(
        [r.sums[0, 0:1], r.sums[1, 0:1], jnp.zeros((LANES - 2, width), F32)], axis=0
    )
    small = jnp.concatenate([dot(r.lifted[...].T, r.grams[...]), gains.T], axis=1)
    if z.inside:
        for j in range(n * SPLIT):
            value = small[j * z.small : (j + 1) * z.small].astype(BF)
            r.sm_part[j % SPLIT, j // SPLIT] = value

        def small_near(slot):
            block = p.t3 if slot else p.t1
            return make_copy(
                r.sm_part.at[block],
                r.sm_near.at[slot],
                r.sm_sem.at[2 * slot],
                r.sm_sem.at[2 * slot + 1],
                tensor=p.t1,
            )

        small_far = make_copy(r.sm_send, r.sm_far, r.sm_sem.at[4], r.sm_sem.at[5], tensor=p.t2)

        def small_copy(step, incoming=False):
            to = peer(step)
            at = to if incoming else p.d
            return make_copy(
                r.sm_out.at[to], r.sm_in.at[at], r.sp_sem.at[0, 0], r.sp_sem.at[1, at], dp=to
            )

        small_near(1).start()
        small_near(0).start()
        small_near(1).wait_recv()
        r.sm_send[...] = (r.sm_part[p.t2].astype(F32) + r.sm_near[1].astype(F32)).astype(BF)
        small_far.start()
    else:
        r.sm_total[...] = small

    pass_copy(0, p.d).start()
    pass_copy(1, p.d).start()
    for step in range(1, n):
        back_copy(step, True).wait_recv()
        pass_copy(1, peer(step)).start()
        pass_copy(0, peer(step)).start()
    if z.inside:
        small_near(0).wait_recv()
        small_far.wait_recv()
        total = r.sm_part[p.t].astype(F32) + r.sm_near[0].astype(F32) + r.sm_far[...].astype(F32)
        r.sm_out[...] = total.astype(BF)
        for step in range(1, n):
            small_copy(step).start()
        r.sm_in[p.d] = r.sm_out[p.d]
        for name in ("dn", "at"):
            for step in range(1, z.groups + 1):
                spreads[name].middle(step)
    for step in range(n):
        of = peer(step)
        pass_copy(1, of, True).wait_recv()
        pass_copy(2, of).start()
    for step in range(n):
        of = peer(step)
        pass_copy(0, of, True).wait_recv()
        pass_copy(2, of, True).wait_recv()
    for i in range(3):
        lid_copy(i, True).wait_recv()
    kept = z.table_rows // SPLIT
    low_table = lane_of((kept, z.pair_width)) < z.table_width

    def add_rows(b, carry):
        block = pl.ds(pl.multiple_of(b * slots, slots), slots)
        arrived = r.back_in[block]
        wanted = row_of((kept, slots)) + p.t * kept
        sums = [dot(onehot(r.lids[b, k][0:1] == wanted), arrived) for k in range(2)]
        r.table_grads[...] += jnp.where(low_table, sums[0], sums[1])
        return carry

    r.table_grads[...] = jnp.zeros_like(r.table_grads)
    lax.fori_loop(0, SPLIT, add_rows, 0)

    if z.inside:
        for step in range(1, n):
            small_copy(step, True).wait_recv()
        r.sm_total[...] = jnp.sum(r.sm_in[...].astype(F32), axis=0)
        for spread in spreads.values():
            spread.finish()

    all_ids.wait_send()
    shared = [(r.rows_out, r.row_sem, cap), (r.back_out, r.back_sem, cap)]
    if z.inside:
        shared.append((r.sm_out, r.sp_sem, 1))
    for ref, sems, each in shared:
        ref = ref.at[pl.ds(0, (n - 1) * each)]
        make_copy(ref, ref, sems.at[0, 0], sems.at[1, 0], dp=peer(1)).wait_send()
    for i in range(3):
        lid_copy(i).wait_send()
    for gather in (gather1, gather2, gather3):
        gather.close()
    for scatter in scatters[1:]:
        scatter.close()
    for spread in spreads.values():
        spread.close()
    if z.inside:
        small_near(0).wait_send()
        small_near(1).wait_send()
        small_far.wait_send()
    for step in range(n):
        for kind in range(3):
            pass_copy(kind, peer(step)).wait_send()


def shards(
    embedded,
    bigram_ids,
    trigram_ids,
    prefix_lens,
    bigram_table,
    trigram_table,
    ngram_weight,
    first_gain,
    attend_weight,
    output_weight,
    second_gain,
    gate_weight,
    up_weight,
    down_weight,
    cotangent,
):
    n = lax.axis_size("dp")
    rows, width = embedded.shape
    table_rows, table_width = bigram_table.shape
    heads, units = attend_weight.shape[1] // (3 * HD), gate_weight.shape[1]
    z = Sizes(n, rows, width, heads, units, table_rows, table_width)
    scratch, outs = scratch_of(z), outputs_of(z)
    names = (*INPUTS, *outs, *scratch)
    anywhere = pl.BlockSpec(memory_space=pl.ANY)
    in_specs = [anywhere] * len(INPUTS)
    in_specs[3] = pl.BlockSpec(memory_space=pltpu.SMEM)
    got = pl.pallas_call(
        functools.partial(block_kernel, z, names),
        out_shape=[jax.ShapeDtypeStruct(*item) for item in outs.values()],
        in_specs=in_specs,
        out_specs=[pl.BlockSpec(memory_space=pltpu.VMEM)] * len(outs),
        scratch_shapes=list(scratch.values()),
        compiler_params=pltpu.CompilerParams(
            collective_id=0, has_side_effects=True, vmem_limit_bytes=67043328
        ),
        name="block",
    )(
        embedded,
        bigram_ids.reshape(1, rows),
        trigram_ids.reshape(1, rows),
        prefix_lens,
        bigram_table,
        trigram_table,
        ngram_weight,
        first_gain.reshape(1, width),
        attend_weight,
        output_weight,
        second_gain.reshape(1, width),
        gate_weight,
        up_weight,
        down_weight,
        cotangent,
    )
    got = dict(zip(outs, got, strict=True))
    tables = got["table_grads"]
    small = got["sm_total"]
    if z.inside:
        gate_up, down, attn = got["gu_out"], got["dn_out"], got["at_out"]
    else:
        gate_up, down, attn = (
            lax.psum_scatter(got[name].astype(F32), "dp", scatter_dimension=0, tiled=True)
            for name in ("gu_part", "dn_part", "at_part")
        )
        small = lax.psum_scatter(small, ("dp", "tensor"), scatter_dimension=0, tiled=True)
    side = 3 * heads * HD
    return (
        got["block_out"],
        got["embed_grad"],
        tables[:, :table_width],
        tables[:, table_width:],
        small[:, : 2 * table_width].T,
        small[:, 2 * table_width],
        attn[:, :side],
        attn[:, side:].T,
        small[:, 2 * table_width + 1],
        gate_up[:, :units],
        gate_up[:, units:],
        down.T,
    )


def solution(mesh):
    placed = (
        P(("dp", "tensor"), None),
        P(("dp", "tensor")),
        P(("dp", "tensor")),
        P("dp"),
        P("dp", None),
        P("dp", None),
        P(),
        P(),
        P(None, "tensor"),
        P("tensor", None),
        P(),
        P(None, "tensor"),
        P(None, "tensor"),
        P("tensor", None),
        P("dp", None),
    )
    return jax.shard_map(
        shards,
        mesh=mesh,
        in_specs=placed,
        out_specs=(
            P(("dp", "tensor"), None),
            P(("dp", "tensor"), None),
            P(("dp", "tensor"), None),
            P(("dp", "tensor"), None),
            P(None, ("dp", "tensor")),
            P(("dp", "tensor")),
            P("dp", "tensor"),
            P("tensor", "dp"),
            P(("dp", "tensor")),
            P("dp", "tensor"),
            P("dp", "tensor"),
            P("tensor", "dp"),
        ),
        check_vma=False,
    )
```

time: 823 us -> 178 us (0.22)
  waiting for transfers between devices: 567 us -> 0 us
  Pallas kernels: 0 us -> 156 us
  matrix products: 64.9 us -> 0 us
  local copies, waits for them, and re-layouts: 77.9 us -> 19.8 us
  other arithmetic: 45 us -> 0 us
  blocking collectives: 25.3 us -> 0 us
  starting transfers between devices: 18 us -> 0 us
  between operations: 16.4 us -> 1.41 us
    reduce_scatter x11 -> x0, waiting for transfers between devices: 412 us -> none  [the longest x1 69.7 us: shards(): lax.psum_scatter(attend_grad, 'dp', scatter_dimension=0, tiled=True)]
    pallas_call x0 -> x1, Pallas kernels: none -> 156 us  [shards(): pl.pallas_call(functools.partial(block_kernel, z, names), out_shape=[jax....]
    unnamed x18 -> x0, waiting for transfers between devices: 65.6 us -> none
    dot_general x33 -> x0, matrix products: 61.7 us -> none  [the longest x5 16 us: inner(): lax.dot_general(left, right, (((0,), (0,)), ((), ())), preferred_element_...]
    all_gather x3 -> x0, waiting for transfers between devices: 57.4 us -> none  [the longest x1 19.8 us: shards(): lax.all_gather(normed_two.astype(jnp.bfloat16), 'tensor', axis=0, tiled=T...]
    scatter x4 -> x0, local copies, waits for them, and re-layouts: 51 us -> none  [the longest x1 13.1 us: shards(): outgoing = outgoing.at[1, trigram_slot].set(row_back[:, table_width:])]
    all_to_all x3 -> x0, waiting for transfers between devices: 31.9 us -> none  [the longest x1 14.3 us: shards(): lax.all_to_all(outgoing.astype(jnp.bfloat16), 'dp', split_axis=1, concat_...]
    unnamed x2 -> x0, blocking collectives: 25.3 us -> none
  transfers between devices with their start and end apart: 19 -> 0, of which waited for: 18 -> 0; matrix products, arithmetic and copies ran while one was open for 9% -> 0% of each run, Pallas kernels for 0% -> 0%
where the time goes in v2:
time: 178 us; the launch traced here: 177 us
  Pallas kernels  156 us (88%)
  local copies, waits for them, and re-layouts  19.8 us (11%)
    pallas_call x1, Pallas kernels, shards(): pl.pallas_call(functools.partial(block_kernel, z, names), out_shape=[jax....  156 us
    unnamed x21, local copies, waits for them, and re-layouts  9.81 us

profile of v2, /device:TPU:0, one launch (start us, length us, event | category | flops | bytes accessed | tf_op | source)
XLA Modules:
  0.0 177.3 jit_solution(9414028189916560680)
XLA Ops:
  0.6 0.0 copy-start.1
  1.4 1.3 reshape.38.refs_7_
  2.6 1.3 reshape.39.refs_10_
  3.9 2.3 %copy.35.refs_8_ = bf16[768,576]{1,0:T(8,128)(2,1)} copy(bf16[768,576]{0,1:T(8,128)(2,1)} %param.23) | data formatting | bytes 1769472 | tf_op args[8]
  6.2 0.0 copy-done.1
  6.2 1.3 copy.33.refs_4_
  7.5 0.0 copy-done.2
  7.5 1.3 copy.34.refs_5_
  8.8 156.0 %block.1 = (bf16[256,768]{1,0:T(8,128)(2,1)}, f32[256,768]{1,0:T(8,128)}, f32[512,384]{1,0:T(8,128)}, f32[96,1024]{1,0:T(8,128)}, f32[96,512]{1,0:T(8,128)}, /*index=5*/f32[96,768]{1,0:T(8,128)}, f32[24,512]{1,0:T(8,128)}) custom-call(bf16[256,768]{1,0:T(8,128)(2,1)} %refs_0_.1, s32[1,256]{1,0:T(1,128)} %bitcast.8, s32[1,256]{1,0:T(1,128)} %bitcast.9, ...), custom_call_target="tpu_custom_call" | custom-call | tf_op jit(solution)/shard_map/block/pallas_call | solution.py:970
  164.8 0.0 copy-start
  164.8 1.5 slice_reduce_fusion
  166.3 1.4 slice_bitcast_fusion.1
  167.7 1.0 slice_bitcast_fusion
  168.7 1.7 slice.31
  170.4 0.7 copy.38
  171.1 1.8 %fusion.1 = (f32[96,512]{1,0:T(8,128)}, f32[96,512]{1,0:T(8,128)}) fusion(f32[96,1024]{1,0:T(8,128)} %get-tuple-element.24), kind=kLoop, calls=%fused_computation.5 | loop fusion | bytes 786432 | tf_op jit(solution)/shard_map/slice | solution.py:1020
  172.9 0.0 copy-done
  172.9 0.2 fusion
  173.1 0.9 copy.37
  174.0 0.9 copy.36
  175.0 0.0 copy-done.4
  175.0 0.7 copy.43
  175.7 0.9 copy.44
  176.6 0.7 copy.45
  (6 shorter events, 0.0 us)
Async XLA Ops:
  0.6 5.6 %copy-start.1 = (bf16[2048,192]{0,1:T(8,128)(2,1)S(1)}, bf16[2048,192]{0,1:T(8,128)(2,1)}, u32[]{:S(2)}) copy-start(bf16[2048,192]{0,1:T(8,128)(2,1)} %param.19) | copy-start | bytes 2359300
  3.9 3.6 %copy-start.2 = (bf16[2048,192]{0,1:T(8,128)(2,1)S(1)}, bf16[2048,192]{0,1:T(8,128)(2,1)}, u32[]{:S(2)}) copy-start(bf16[2048,192]{0,1:T(8,128)(2,1)} %param.20) | copy-start | bytes 2359300
  164.8 8.1 %copy-start = (f32[512,384]{1,0:T(8,128)S(1)}, f32[512,384]{1,0:T(8,128)}, u32[]{:S(2)}) copy-start(f32[512,384]{1,0:T(8,128)} %get-tuple-element.21) | copy-start | bytes 2359300
  172.9 2.1 %copy-start.4 = (bf16[256,768]{1,0:T(8,128)(2,1)S(1)}, bf16[256,768]{1,0:T(8,128)(2,1)}, u32[]{:S(2)}) copy-start(bf16[256,768]{1,0:T(8,128)(2,1)} %get-tuple-element.68) | copy-start | bytes 1179652
  173.1 2.6 %copy-start.3 = (f32[256,768]{1,0:T(8,128)S(1)}, f32[256,768]{1,0:T(8,128)}, u32[]{:S(2)}) copy-start(f32[256,768]{1,0:T(8,128)} %get-tuple-element.69) | copy-start | bytes 2359300
  174.0 2.6 %copy-start.5 = (f32[96,512]{1,0:T(8,128)S(1)}, f32[96,512]{1,0:T(8,128)}, u32[]{:S(2)}) copy-start(f32[96,512]{1,0:T(8,128)} %get-tuple-element.25) | copy-start | bytes 589828

commit v3 on v2

--- a/solution.py
+++ b/solution.py
@@ -71,7 +71,7 @@
         self.pair_width = 2 * table_width
         self.small = width // (n * SPLIT)
         self.small_lanes = self.pair_width + LANES
-        self.attn_lanes = heads * HD * 4
+        self.attn_lanes = 4 * HD
         self.inside = self.piece % 16 == 0 and self.small % 8 == 0
 
 
@@ -249,14 +249,12 @@
         emb=vmem((rows, width), BF),
         ids=vmem((2 * n, 1, rows), jnp.int32),
         own_ids=vmem((2, 1, rows), jnp.int32),
-        table_b=vmem((z.table_rows, z.table_width), BF),
-        table_t=vmem((z.table_rows, z.table_width), BF),
+        table_b=vmem((z.table_width, z.table_rows), BF),
+        table_t=vmem((z.table_width, z.table_rows), BF),
         nw=vmem((z.pair_width, width), BF),
-        gain1=vmem((1, width), F32),
-        gain2=vmem((1, width), F32),
-        wa=vmem((width, 3 * z.heads * HD), BF),
-        wap=vmem((width, 3 * z.padded), BF),
-        wo=vmem((z.heads * HD, width), BF),
+        gain1=vmem((width,), F32),
+        gain2=vmem((width,), F32),
+        wap=vmem((3 * z.padded, width), BF),
         wop=vmem((z.padded, width), BF),
         wgu=vmem((width, 2 * z.units), BF),
         wd=vmem((z.units, width), BF),
@@ -286,8 +284,10 @@
         probs3=vmem((z.heads, rows, z.keys[3]), BF),
         att=vmem((length, z.padded), BF),
         do=vmem((length, z.padded), BF),
-        dk=vmem((z.heads, HD, length), F32),
-        dv=vmem((z.heads, HD, length), F32),
+        dk=vmem((HD, length), F32),
+        dv=vmem((HD, length), F32),
+        n1t=vmem((width, length), BF),
+        abt=vmem((width, length), BF),
         mixb=vmem((length, 3 * z.padded), BF),
         act=vmem((length, z.units), BF),
         gub=vmem((length, 2 * z.units), BF),
@@ -295,7 +295,7 @@
         sums=vmem((2, 8, width), F32),
         back_out=vmem((z.slots, z.pair_width), BF),
         back_in=vmem((SPLIT * z.slots, z.pair_width), BF),
-        in_sem=dma((16,)),
+        in_sem=dma((12 + 4 * z.heads,)),
         id_sem=dma((2,)),
         row_sem=dma((2, n)),
         lid_sem=dma((2, 3)),
@@ -313,7 +313,8 @@
         shapes[f"rs{k}_sem"] = dma((chunks, 6))
     shapes["rs4_sem"] = dma((chunks, 6))
     if z.inside:
-        for name, lanes in (("gu", 2 * z.units), ("dn", z.units), ("at", z.attn_lanes)):
+        heads = [(f"at{h}", z.attn_lanes) for h in range(z.heads)]
+        for name, lanes in (("gu", 2 * z.units), ("dn", z.units), *heads):
             shapes[f"{name}_part"] = vmem((width, lanes), BF)
             shapes[f"{name}_pair_in"] = vmem((z.groups, z.piece, lanes), BF)
             shapes[f"{name}_pair_out"] = vmem((z.groups - 1, z.piece, lanes), BF)
@@ -341,12 +342,14 @@
     if z.inside:
         shapes["gu_out"] = ((z.piece, 2 * z.units), F32)
         shapes["dn_out"] = ((z.piece, z.units), F32)
-        shapes["at_out"] = ((z.piece, z.attn_lanes), F32)
+        for h in range(z.heads):
+            shapes[f"at{h}_out"] = ((z.piece, z.attn_lanes), F32)
         shapes["sm_total"] = ((z.small, z.small_lanes), F32)
     else:
         shapes["gu_part"] = ((width, 2 * z.units), BF)
         shapes["dn_part"] = ((width, z.units), BF)
-        shapes["at_part"] = ((width, z.attn_lanes), BF)
+        for h in range(z.heads):
+            shapes[f"at{h}_part"] = ((width, z.attn_lanes), BF)
         shapes["sm_total"] = ((width, z.small_lanes), F32)
     return shapes
 
@@ -369,7 +372,7 @@
     scatter1, scatter2, scatter3, scatter4 = scatters
     spreads = {}
     if z.inside:
-        for name in ("gu", "dn", "at"):
+        for name in ("gu", "dn", *(f"at{h}" for h in range(heads))):
             spreads[name] = Spread(
                 z, p, getattr(r, f"{name}_part"), getattr(r, f"{name}_pair_in"),
                 getattr(r, f"{name}_pair_out"), getattr(r, f"{name}_far_in"),
@@ -390,8 +393,6 @@
         (r.trigram_ids, r.own_ids.at[1]),
         (r.bigram_table, r.table_b),
         (r.trigram_table, r.table_t),
-        (r.attend_weight, r.wa),
-        (r.output_weight, r.wo),
         (r.embedded, r.emb),
         (r.ngram_weight, r.nw),
         (r.first_gain, r.gain1),
@@ -401,6 +402,12 @@
         (r.down_weight, r.wd),
         (r.cotangent, r.cot),
     ]
+    for h in range(heads):
+        for c in range(3):
+            src = r.attend_weight.at[pl.ds((3 * h + c) * HD, HD)]
+            loads.append((src, r.wap.at[pl.ds(c * padded + h * LANES, HD)]))
+        src = r.output_weight.at[pl.ds(h * HD, HD)]
+        loads.append((src, r.wop.at[pl.ds(h * LANES, HD)]))
     loads = [pltpu.make_async_copy(src, dst, r.in_sem.at[i]) for i, (src, dst) in enumerate(loads)]
     for load in loads:
         load.start()
@@ -452,24 +459,12 @@
         across = jnp.broadcast_to(slot, (rows, LANES)).T[0:1]
         r.pick_t[k] = onehot(across.astype(jnp.int32) == row_of((slots, rows)))
 
-    loads[4].wait()
-    low_half = lane_of((width, LANES)) < HD
     for h in range(heads):
+        empty = jnp.zeros((LANES - HD, width), BF)
         for c in range(3):
-            at = (3 * h + c) * HD
-            block = r.wa[:, at // LANES * LANES : min(at // LANES * LANES + LANES, 3 * heads * HD)]
-            block = block.astype(F32)
-            if block.shape[1] < LANES:
-                fill = jnp.zeros((width, LANES - block.shape[1]), F32)
-                block = jnp.concatenate([block, fill], axis=1)
-            if at % LANES:
-                block = roll64(block)
-            to = c * padded + h * LANES
-            r.wap[:, to : to + LANES] = jnp.where(low_half, block, 0.0).astype(BF)
-    loads[5].wait()
-    for h in range(heads):
-        r.wop[h * LANES : h * LANES + HD] = r.wo[h * HD : (h + 1) * HD]
-        r.wop[h * LANES + HD : (h + 1) * LANES] = jnp.zeros((HD, width), BF)
+            at = c * padded + h * LANES + HD
+            r.wap[at : at + LANES - HD] = empty
+        r.wop[h * LANES + HD : (h + 1) * LANES] = empty
 
     loads[2].wait()
     loads[3].wait()
@@ -516,7 +511,7 @@
         for k, table in enumerate((r.table_b, r.table_t)):
             chosen = picked[k][part * half : (part + 1) * half]
             hits = onehot(chosen == lane_of((half, z.table_rows)))
-            both = dot(hits, table[...])
+            both = dot_right(hits, table[...])
             fill = jnp.zeros((half, 2 * LANES - z.table_width), F32)
             found.append((both[:, :LANES], jnp.concatenate([both[:, LANES:], fill], axis=1)))
         low_half = lane_of((half, LANES)) < HD
@@ -531,7 +526,7 @@
     own_slots = pl.ds(pl.multiple_of(p.d * cap, cap), cap)
     r.rows_in[own_slots] = r.rows_out[own_slots]
 
-    for load in loads[6:10]:
+    for load in loads[4:8]:
         load.wait()
     for step in range(1, n):
         row_arrival(step).wait_recv()
@@ -544,7 +539,7 @@
     scale = lax.rsqrt(jnp.mean(inputs * inputs, axis=1, keepdims=True) + 1e-05)
     r.scale1[...] = jnp.broadcast_to(scale, (rows, LANES))
     own_rows = pl.ds(pl.multiple_of(p.t * rows, rows), rows)
-    r.n1[own_rows] = (inputs * scale * r.gain1[...]).astype(BF)
+    r.n1[own_rows] = (inputs * scale * r.gain1[...][None, :]).astype(BF)
     for c in range(CHUNKS):
         gather1.send(c)
 
@@ -568,9 +563,12 @@
         for b, span in enumerate(spans(c)):
             ref[(span, *rest)] = value[b * z.chunk : (b + 1) * z.chunk]
 
+    for load in loads[8:]:
+        load.wait()
+
     def project(c, carry):
         gather1.receive(c)
-        mixture = dot(take(r.n1, c), r.wap[...])
+        mixture = dot_right(take(r.n1, c), r.wap[...])
         cosine, sines = take(r.cosine, c), take(r.sines, c)
         for h in range(heads):
             for i, (ref, factor) in enumerate(((r.q, HD**-0.5), (r.k, 1.0))):
@@ -618,9 +616,6 @@
     for c in range(CHUNKS):
         scatter1.middle(c)
 
-    for load in loads[10:]:
-        load.wait()
-
     def second_norm(c, carry):
         span = scatter1.span(c)
         after = r.inputs[span] + scatter1.finish(c)
@@ -628,7 +623,7 @@
         scale = lax.rsqrt(jnp.mean(after * after, axis=1, keepdims=True) + 1e-05)
         r.scale2[span] = jnp.broadcast_to(scale, (z.chunk, LANES))
         own = scatter1.rows(p.t, c)
-        r.n2[own] = (after * scale * r.gain2[...]).astype(BF)
+        r.n2[own] = (after * scale * r.gain2[...][None, :]).astype(BF)
         gather2.send(c)
         return carry
 
@@ -677,7 +672,7 @@
     def second_back(c, carry):
         span = scatter3.span(c)
         grad = scatter3.finish(c)
-        row_grad, total = norm_back(grad, r.after[span], r.scale2[span, 0:1], r.gain2[...])
+        row_grad, total = norm_back(grad, r.after[span], r.scale2[span, 0:1], r.gain2[...][None, :])
         r.sums[1, 0:1] += total
         own = scatter3.rows(p.t, c)
         after_grad = r.cot[own].astype(F32) + row_grad
@@ -712,34 +707,96 @@
         return carry
 
     lax.fori_loop(0, CHUNKS, attended_back, 0)
-    r.dk[...] = jnp.zeros_like(r.dk)
-    r.dv[...] = jnp.zeros_like(r.dv)
 
     def unrotate(grads, span):
         grads = grads.astype(BF).astype(F32)
         turned = grads * r.cosine[span] - swap_halves(grads) * r.sines[span]
         return turned.astype(BF)
 
-    def attend_back(first, keys, kept):
-        span = slice(first, first + rows)
-
-        def one_head(h, carry):
-            at = head_lanes(h)
-            do, q = r.do[span, at], r.q[span, at]
-            weights = kept[h]
-            prob_back = dot_right(do, r.v[0:keys, at])
-            centre = jnp.sum(do.astype(F32) * r.att[span, at].astype(F32), axis=1, keepdims=True)
-            score_back = (weights.astype(F32) * (prob_back - centre)).astype(BF)
-            query_back = dot(score_back, r.k[0:keys, at]) * HD**-0.5
-            r.mixb[span, at] = unrotate(query_back, span)
-            r.dk[h, :, 0:keys] += dot(q.T[:HD], score_back)
-            r.dv[h, :, 0:keys] += dot(do.T[:HD], weights)
+    def upright(block):
+        return jnp.concatenate([block, jnp.zeros_like(block)], axis=0).T
+
+    def attend_back(h, first, keys, kept, whole):
+        span, at = slice(first, first + rows), slice(h * LANES, (h + 1) * LANES)
+        do, q = r.do[span, at], r.q[span, at]
+        weights = kept[h]
+        prob_back = dot_right(do, r.v[0:keys, at])
+        centre = jnp.sum(do.astype(F32) * r.att[span, at].astype(F32), axis=1, keepdims=True)
+        score_back = (weights.astype(F32) * (prob_back - centre)).astype(BF)
+        query_back = dot(score_back, r.k[0:keys, at]) * HD**-0.5
+        r.mixb[span, at] = unrotate(query_back, span)
+        key_back, value_back = dot(q.T[:HD], score_back), dot(do.T[:HD], weights)
+        if whole:
+            r.dk[...] = key_back
+            r.dv[...] = value_back
+        else:
+            r.dk[:, 0:keys] += key_back
+            r.dv[:, 0:keys] += value_back
+
+    def turned_tile(j, carry):
+        at = pl.ds(pl.multiple_of(j * tile, tile), tile)
+        r.n1t[at] = r.n1[:, at].T
+        r.abt[at] = r.ab[:, at].T
+        return carry
+
+    lax.fori_loop(0, width // tile, turned_tile, 0)
+
+    def head_tiles(h):
+        part = getattr(r, f"at{h}_part")
+        lanes = [slice(c * padded + h * LANES, c * padded + (h + 1) * LANES) for c in range(3)]
+
+        def head_tile(j, carry):
+            at = pl.ds(pl.multiple_of(j * tile, tile), tile)
+            mixed = jnp.concatenate([r.mixb[:, span] for span in lanes], axis=1)
+            grad = dot(r.n1t[at], mixed)
+            outer = dot(r.abt[at], r.att[:, h * LANES : (h + 1) * LANES])
+            first = grad[:, :LANES] + roll64(grad[:, LANES : 2 * LANES])
+            second = grad[:, 2 * LANES :] + roll64(outer)
+            part[at, 0:LANES] = first.astype(BF)
+            part[at, LANES:] = second.astype(BF)
             return carry
 
-        lax.fori_loop(0, heads, one_head, 0)
-
-    for block in blocks:
-        attend_back(*block)
+        lax.fori_loop(0, width // tile, head_tile, 0)
+
+    waiting = [("gu", i) for i in range(1, z.groups + 1)] + [("dn", i) for i in range(1, z.groups + 1)]
+
+    def pair_sums(count):
+        for name, step in waiting[:count]:
+            if z.inside:
+                spreads[name].middle(step)
+        del waiting[:count]
+
+    pair_sums(2 * z.groups // 4)
+    for h in range(heads):
+        for i in reversed(range(SPLIT)):
+            first, keys, kept = blocks[i]
+            attend_back(h, first, keys, kept, i == SPLIT - 1)
+            pair_sums(1)
+        for i in range(SPLIT):
+            span = slice(i * rows, (i + 1) * rows)
+            at = padded + h * LANES
+            r.mixb[span, at : at + LANES] = unrotate(upright(r.dk[:, span]), span)
+            at = 2 * padded + h * LANES
+            r.mixb[span, at : at + LANES] = upright(r.dv[:, span]).astype(BF)
+        if h < heads - 1:
+            head_tiles(h)
+            if z.inside:
+                spreads[f"at{h}"].send()
+                waiting.extend((f"at{h}", i) for i in range(1, z.groups + 1))
+    scatter1.close()
+
+    def first_norm_part(c, carry):
+        put(r.part1, c, dot(take(r.mixb, c), r.wap[...]).astype(BF))
+        scatter4.send(c)
+        return carry
+
+    lax.fori_loop(0, CHUNKS, first_norm_part, 0)
+    for c in range(CHUNKS):
+        scatter4.middle(c)
+    head_tiles(heads - 1)
+    if z.inside:
+        spreads[f"at{heads - 1}"].send()
+    pair_sums(len(waiting))
 
     def block_out(c, carry):
         span = scatter2.span(c)
@@ -748,54 +805,10 @@
 
     lax.fori_loop(0, CHUNKS, block_out, 0)
 
-    def upright(block):
-        return jnp.concatenate([block, jnp.zeros_like(block)], axis=0).T
-
-    scatter1.close()
-    for h in range(heads):
-        for i in range(SPLIT):
-            span = slice(i * rows, (i + 1) * rows)
-            at = padded + h * LANES
-            r.mixb[span, at : at + LANES] = unrotate(upright(r.dk[h, :, span]), span)
-            at = 2 * padded + h * LANES
-            r.mixb[span, at : at + LANES] = upright(r.dv[h, :, span]).astype(BF)
-
-    def first_norm_part(c, carry):
-        put(r.part1, c, dot_right(take(r.mixb, c), r.wap[...]).astype(BF))
-        scatter4.send(c)
-        return carry
-
-    lax.fori_loop(0, CHUNKS, first_norm_part, 0)
-    for c in range(CHUNKS):
-        scatter4.middle(c)
-    if z.inside:
-        for step in range(1, z.groups + 1):
-            spreads["gu"].middle(step)
-
-    def attend_tile(j, carry):
-        at = pl.ds(pl.multiple_of(j * tile, tile), tile)
-        grad = dot(r.n1[:, at].T, r.mixb[...])
-        outer = dot(r.ab[:, at].T, r.att[...])
-        parts = []
-        for h in range(heads):
-            for c in range(3):
-                start = c * padded + h * LANES
-                parts.append(grad[:, start : start + LANES])
-        for h in range(heads):
-            parts.append(outer[:, h * LANES : (h + 1) * LANES])
-        for g in range(len(parts) // 2):
-            both = parts[2 * g] + roll64(parts[2 * g + 1])
-            r.at_part[at, g * LANES : (g + 1) * LANES] = both.astype(BF)
-        return carry
-
-    lax.fori_loop(0, width // tile, attend_tile, 0)
-    if z.inside:
-        spreads["at"].send()
-
     def first_back(c, carry):
         span = scatter4.span(c)
         grad = scatter4.finish(c)
-        row_grad, total = norm_back(grad, r.inputs[span], r.scale1[span, 0:1], r.gain1[...])
+        row_grad, total = norm_back(grad, r.inputs[span], r.scale1[span, 0:1], r.gain1[...][None, :])
         r.sums[0, 0:1] += total
         embed_grad = r.aftergrad[span] + row_grad
         r.embed_grad[span] = embed_grad
@@ -882,32 +895,36 @@
         for step in range(1, n):
             small_copy(step).start()
         r.sm_in[p.d] = r.sm_out[p.d]
-        for name in ("dn", "at"):
-            for step in range(1, z.groups + 1):
-                spreads[name].middle(step)
+        for step in range(1, z.groups + 1):
+            spreads[f"at{heads - 1}"].middle(step)
     for step in range(n):
         of = peer(step)
         pass_copy(1, of, True).wait_recv()
         pass_copy(2, of).start()
-    for step in range(n):
-        of = peer(step)
-        pass_copy(0, of, True).wait_recv()
-        pass_copy(2, of, True).wait_recv()
     for i in range(3):
         lid_copy(i, True).wait_recv()
     kept = z.table_rows // SPLIT
-    low_table = lane_of((kept, z.pair_width)) < z.table_width
-
-    def add_rows(b, carry):
+    low_table = lane_of((kept, LANES)) < HD
+    wanted = row_of((kept, slots)) + p.t * kept
+
+    def add_rows(b, fresh=False):
         block = pl.ds(pl.multiple_of(b * slots, slots), slots)
-        arrived = r.back_in[block]
-        wanted = row_of((kept, slots)) + p.t * kept
-        sums = [dot(onehot(r.lids[b, k][0:1] == wanted), arrived) for k in range(2)]
-        r.table_grads[...] += jnp.where(low_table, sums[0], sums[1])
-        return carry
-
-    r.table_grads[...] = jnp.zeros_like(r.table_grads)
-    lax.fori_loop(0, SPLIT, add_rows, 0)
+        hits = [onehot(r.lids[b, k][0:1] == wanted) for k in range(2)]
+        left = dot(hits[0], r.back_in[block, 0 : 2 * LANES])
+        right = dot(hits[1], r.back_in[block, LANES : 3 * LANES])
+        sums = (left[:, :LANES], jnp.where(low_table, left[:, LANES:], right[:, :LANES]), right[:, LANES:])
+        for g, value in enumerate(sums):
+            at = slice(g * LANES, (g + 1) * LANES)
+            r.table_grads[:, at] = value if fresh else r.table_grads[:, at] + value
+
+    add_rows(p.t, True)
+    for step in range(n):
+        pass_copy(0, peer(step), True).wait_recv()
+    add_rows(p.t1)
+    add_rows(p.t2)
+    for step in range(n):
+        pass_copy(2, peer(step), True).wait_recv()
+    add_rows(p.t3)
 
     if z.inside:
         for step in range(1, n):
@@ -938,6 +955,57 @@
     for step in range(n):
         for kind in range(3):
             pass_copy(kind, peer(step)).wait_send()
+
+
+def finish_kernel(z, names, *refs):
+    r = Refs(names, refs)
+    r.block[...] = r.block_out[...]
+    r.embed[...] = r.embed_grad[...]
+    r.bigram[...] = r.table_grads[:, : 2 * LANES].T[: z.table_width]
+    r.trigram[...] = r.table_grads[:, LANES:].T[2 * LANES - z.table_width :]
+    r.ngram[...] = r.sm_total[:, : z.pair_width]
+    gains = r.sm_total[:, z.pair_width :]
+    r.first[...] = gains[:, 0:1].T
+    r.second[...] = gains[:, 1:2].T
+    r.gate[...] = r.gu_out[:, : z.units]
+    r.up[...] = r.gu_out[:, z.units :]
+    r.down[...] = r.dn_out[...]
+    side = 3 * HD
+    for h in range(z.heads):
+        sums = getattr(r, f"at{h}_out")[...]
+        r.attend[:, h * side : (h + 1) * side] = sums[:, :side]
+        r.output[h * HD : (h + 1) * HD] = sums[:, LANES:].T[HD:]
+
+
+def finish_outputs(z, got):
+    kept = z.table_rows // SPLIT
+    outs = dict(
+        block=((z.rows, z.width), BF),
+        embed=((z.rows, z.width), F32),
+        bigram=((z.table_width, kept), F32),
+        trigram=((z.table_width, kept), F32),
+        ngram=((z.small, z.pair_width), F32),
+        first=((1, z.small), F32),
+        attend=((z.piece, 3 * HD * z.heads), F32),
+        output=((HD * z.heads, z.piece), F32),
+        second=((1, z.small), F32),
+        gate=((z.piece, z.units), F32),
+        up=((z.piece, z.units), F32),
+        down=((z.piece, z.units), F32),
+    )
+    done = pl.pallas_call(
+        functools.partial(finish_kernel, z, (*got, *outs)),
+        out_shape=[jax.ShapeDtypeStruct(*item) for item in outs.values()],
+        in_specs=[pl.BlockSpec(memory_space=pltpu.VMEM)] * len(got),
+        out_specs=[pl.BlockSpec(memory_space=pltpu.VMEM)] * len(outs),
+        name="finish",
+    )(*got.values())
+    done = dict(zip(outs, done, strict=True))
+    for name in ("bigram", "trigram", "ngram", "down"):
+        done[name] = done[name].T
+    for name in ("first", "second"):
+        done[name] = done[name].reshape(z.small)
+    return tuple(done.values())
 
 
 def shards(
@@ -982,44 +1050,28 @@
         bigram_ids.reshape(1, rows),
         trigram_ids.reshape(1, rows),
         prefix_lens,
-        bigram_table,
-        trigram_table,
+        bigram_table.T,
+        trigram_table.T,
         ngram_weight,
-        first_gain.reshape(1, width),
-        attend_weight,
+        first_gain,
+        attend_weight.T,
         output_weight,
-        second_gain.reshape(1, width),
+        second_gain,
         gate_weight,
         up_weight,
         down_weight,
         cotangent,
     )
     got = dict(zip(outs, got, strict=True))
-    tables = got["table_grads"]
-    small = got["sm_total"]
-    if z.inside:
-        gate_up, down, attn = got["gu_out"], got["dn_out"], got["at_out"]
-    else:
-        gate_up, down, attn = (
-            lax.psum_scatter(got[name].astype(F32), "dp", scatter_dimension=0, tiled=True)
-            for name in ("gu_part", "dn_part", "at_part")
-        )
-        small = lax.psum_scatter(small, ("dp", "tensor"), scatter_dimension=0, tiled=True)
-    side = 3 * heads * HD
-    return (
-        got["block_out"],
-        got["embed_grad"],
-        tables[:, :table_width],
-        tables[:, table_width:],
-        small[:, : 2 * table_width].T,
-        small[:, 2 * table_width],
-        attn[:, :side],
-        attn[:, side:].T,
-        small[:, 2 * table_width + 1],
-        gate_up[:, :units],
-        gate_up[:, units:],
-        down.T,
-    )
+    if not z.inside:
+
+        def summed(part, axes):
+            return lax.psum_scatter(part, axes, scatter_dimension=0, tiled=True)
+
+        for name in ("gu", "dn", *(f"at{h}" for h in range(heads))):
+            got[f"{name}_out"] = summed(got.pop(f"{name}_part").astype(F32), "dp")
+        got["sm_total"] = summed(got["sm_total"], ("dp", "tensor"))
+    return finish_outputs(z, got)
 
 
 def solution(mesh):

time: 178 us -> 155 us (0.87)
  local copies, waits for them, and re-layouts: 19.8 us -> 0 us
  Pallas kernels: 156 us -> 154 us
    unnamed x21 -> x0, local copies, waits for them, and re-layouts: 9.81 us -> none
    pallas_call x1, Pallas kernels: 156 us -> 150 us  [shards(): pl.pallas_call(functools.partial(block_kernel, z, names), out_shape=[jax....]
    slice x4 -> x0, local copies, waits for them, and re-layouts: 5.14 us -> none  [the longest x1 1.79 us: shards(): gate_up[:, units:]]
    pallas_call x0 -> x1, Pallas kernels: none -> 3.75 us  [finish_outputs(): pl.pallas_call(functools.partial(finish_kernel, z, (*got, *outs)), out_sh...]
    reshape x2 -> x0, local copies, waits for them, and re-layouts: 2.53 us -> none  [the longest x1 1.27 us: shards(): first_gain.reshape(1, width)]
    transpose x2 -> x0, local copies, waits for them, and re-layouts: 2.36 us -> none  [the longest x1 1.39 us: shards(): small[:, :2 * table_width]]
where the time goes in v3:
time: 155 us
  Pallas kernels  154 us (99%)
    pallas_call x1, Pallas kernels, shards(): pl.pallas_call(functools.partial(block_kernel, z, names), out_shape=[jax....  150 us
    pallas_call x1, Pallas kernels, finish_outputs(): pl.pallas_call(functools.partial(finish_kernel, z, (*got, *outs)), out_sh...  3.75 us

profile of v3, /device:TPU:0, one launch (start us, length us, event | category | flops | bytes accessed | tf_op | source)
XLA Modules:
  0.0 155.1 jit_solution(8975659207009684393)
XLA Ops:
  1.3 150.0 %block.1 = (bf16[256,768]{1,0:T(8,128)(2,1)}, f32[256,768]{1,0:T(8,128)}, f32[512,384]{1,0:T(8,128)}, f32[96,1024]{1,0:T(8,128)}, f32[96,512]{1,0:T(8,128)}, /*i...) custom-call(bf16[256,768]{1,0:T(8,128)(2,1)} %refs_0_.1, s32[1,256]{1,0:T(1,128)} %bitcast.14, ...), custom_call_target="tpu_custom_call" | custom-call | tf_op jit(solution)/shard_map/block/pallas_call | solution.py:1038
  151.3 3.8 %finish.1 = (bf16[256,768]{1,0:T(8,128)(2,1)}, f32[256,768]{1,0:T(8,128)}, f32[192,512]{1,0:T(8,128)}, f32[192,512]{1,0:T(8,128)}, f32[24,384]{1,0:T(8,128)}, /*...) custom-call(bf16[256,768]{1,0:T(8,128)(2,1)} %get-tuple-element.33.r, ...), custom_call_target="tpu_custom_call" | custom-call | tf_op jit(solution)/shard_map/finish/pallas_call | solution.py:996

commit v4 on v3

--- a/solution.py
+++ b/solution.py
@@ -67,12 +67,11 @@
         self.padded = heads * LANES
         self.chunk = rows // CHUNKS
         self.piece = width // n
-        self.groups = n // 2
         self.pair_width = 2 * table_width
         self.small = width // (n * SPLIT)
         self.small_lanes = self.pair_width + LANES
         self.attn_lanes = 4 * HD
-        self.inside = self.piece % 16 == 0 and self.small % 8 == 0
+        self.inside = n == 8 and self.piece % 16 == 0 and self.small % 8 == 0
 
 
 def make_copy(src, dst, send, recv, **where):
@@ -130,7 +129,7 @@
         return pl.ds(start, self.z.chunk)
 
     def near_copy(self, slot, c):
-        block = self.pos.t3 if slot else self.pos.t1
+        block = self.pos.t1 + slot * (self.pos.t3 - self.pos.t1)
         return make_copy(
             self.part.at[self.rows(block, c)],
             self.near.at[slot, self.span(c)],
@@ -176,59 +175,64 @@
 
 
 class Spread:
-    def __init__(self, z, pos, part, pair_in, pair_out, far_in, out, sems):
+    STEPS = 4
+
+    def __init__(self, z, pos, part, pair_in, next_out, next_in, out, sems):
         self.z, self.pos, self.part, self.pair_in = z, pos, part, pair_in
-        self.pair_out, self.far_in, self.out, self.sems = pair_out, far_in, out, sems
-
-    def group(self, step):
-        return lax.rem(self.pos.place + step, self.z.groups)
+        self.next_out, self.next_in, self.out, self.sems = next_out, next_in, out, sems
+        near = pos.place + 1 - 2 * lax.rem(pos.place, 2)
+        far = lax.rem(pos.place + 2, 4)
+        both = lax.rem(near + 2, 4)
+        self.order = (both, near, far, pos.place)
 
     def rows(self, peer):
         return pl.ds(pl.multiple_of(peer * self.z.piece, self.z.piece), self.z.piece)
 
-    def near_copy(self, step):
-        group = self.group(step)
+    def pair_copy(self, step):
         return make_copy(
-            self.part.at[self.rows(group * 2 + 1 - self.pos.parity)],
-            self.pair_in.at[step - 1],
-            self.sems.at[0, step - 1],
-            self.sems.at[1, step - 1],
+            self.part.at[self.rows(self.order[step] * 2 + 1 - self.pos.parity)],
+            self.pair_in.at[step],
+            self.sems.at[0, step],
+            self.sems.at[1, step],
             dp=self.pos.partner,
         )
 
-    def far_copy(self, step):
+    def next_copy(self, step):
+        place = self.order[1] if step < 2 else self.order[2]
         return make_copy(
-            self.pair_out.at[step - 1],
-            self.far_in.at[step - 1],
-            self.sems.at[2, step - 1],
-            self.sems.at[3, step - 1],
-            dp=self.group(step) * 2 + self.pos.parity,
+            self.next_out.at[step],
+            self.next_in.at[step],
+            self.sems.at[2, step],
+            self.sems.at[3, step],
+            dp=place * 2 + self.pos.parity,
         )
 
     def send(self):
-        for step in range(1, self.z.groups + 1):
-            self.near_copy(step).start()
+        for step in range(4):
+            self.pair_copy(step).start()
 
     def middle(self, step):
-        self.near_copy(step).wait_recv()
-        own = self.part[self.rows(self.group(step) * 2 + self.pos.parity)].astype(F32)
-        total = own + self.pair_in[step - 1].astype(F32)
-        if step == self.z.groups:
+        self.pair_copy(step).wait_recv()
+        own = self.part[self.rows(self.order[step] * 2 + self.pos.parity)].astype(F32)
+        total = own + self.pair_in[step].astype(F32)
+        if step >= 2:
+            self.next_copy(step - 2).wait_recv()
+            total = total + self.next_in[step - 2].astype(F32)
+        if step == 3:
             self.out[...] = total
         else:
-            self.pair_out[step - 1] = total.astype(BF)
-            self.far_copy(step).start()
+            self.next_out[step] = total.astype(BF)
+            self.next_copy(step).start()
 
     def finish(self):
-        for step in range(1, self.z.groups):
-            self.far_copy(step).wait_recv()
-            self.out[...] += self.far_in[step - 1].astype(F32)
+        self.next_copy(2).wait_recv()
+        self.out[...] += self.next_in[2].astype(F32)
 
     def close(self):
-        for step in range(1, self.z.groups + 1):
-            self.near_copy(step).wait_send()
-            if step < self.z.groups:
-                self.far_copy(step).wait_send()
+        for step in range(4):
+            self.pair_copy(step).wait_send()
+            if step < 3:
+                self.next_copy(step).wait_send()
 
 
 class Position:
@@ -270,6 +274,7 @@
         inputs=vmem((rows, width), F32),
         after=vmem((rows, width), F32),
         aftergrad=vmem((rows, width), F32),
+        inverse=vmem((length, LANES), F32),
         scale1=vmem((rows, LANES), F32),
         scale2=vmem((rows, LANES), F32),
         n1=vmem((length, width), BF),
@@ -286,11 +291,9 @@
         do=vmem((length, z.padded), BF),
         dk=vmem((HD, length), F32),
         dv=vmem((HD, length), F32),
-        n1t=vmem((width, length), BF),
-        abt=vmem((width, length), BF),
         mixb=vmem((length, 3 * z.padded), BF),
         act=vmem((length, z.units), BF),
-        gub=vmem((length, 2 * z.units), BF),
+        gub=vmem((max(length, width), 2 * z.units), BF),
         lifted=vmem((rows, width), BF),
         sums=vmem((2, 8, width), F32),
         back_out=vmem((z.slots, z.pair_width), BF),
@@ -316,10 +319,10 @@
         heads = [(f"at{h}", z.attn_lanes) for h in range(z.heads)]
         for name, lanes in (("gu", 2 * z.units), ("dn", z.units), *heads):
             shapes[f"{name}_part"] = vmem((width, lanes), BF)
-            shapes[f"{name}_pair_in"] = vmem((z.groups, z.piece, lanes), BF)
-            shapes[f"{name}_pair_out"] = vmem((z.groups - 1, z.piece, lanes), BF)
-            shapes[f"{name}_far_in"] = vmem((z.groups - 1, z.piece, lanes), BF)
-            shapes[f"{name}_sem"] = dma((4, z.groups))
+            shapes[f"{name}_pair_in"] = vmem((4, z.piece, lanes), BF)
+            shapes[f"{name}_next_out"] = vmem((3, z.piece, lanes), BF)
+            shapes[f"{name}_next_in"] = vmem((3, z.piece, lanes), BF)
+            shapes[f"{name}_sem"] = dma((4, 4))
         small = (n, z.small, z.small_lanes)
         shapes["sm_part"] = vmem((SPLIT, *small), BF)
         shapes["sm_near"] = vmem((2, *small), BF)
@@ -375,7 +378,7 @@
         for name in ("gu", "dn", *(f"at{h}" for h in range(heads))):
             spreads[name] = Spread(
                 z, p, getattr(r, f"{name}_part"), getattr(r, f"{name}_pair_in"),
-                getattr(r, f"{name}_pair_out"), getattr(r, f"{name}_far_in"),
+                getattr(r, f"{name}_next_out"), getattr(r, f"{name}_next_in"),
                 getattr(r, f"{name}_out"), getattr(r, f"{name}_sem"),
             )
 
@@ -571,14 +574,17 @@
         mixture = dot_right(take(r.n1, c), r.wap[...])
         cosine, sines = take(r.cosine, c), take(r.sines, c)
         for h in range(heads):
-            for i, (ref, factor) in enumerate(((r.q, HD**-0.5), (r.k, 1.0))):
+            for i, ref in enumerate((r.q, r.k)):
                 at = i * padded + h * LANES
                 block = mixture[:, at : at + LANES]
-                turned = (block * cosine + swap_halves(block) * sines).astype(BF)
-                if factor != 1.0:
-                    turned = (turned.astype(F32) * factor).astype(BF)
-                put(ref, c, turned, slice(h * LANES, (h + 1) * LANES))
-        put(r.v, c, mixture[:, 2 * padded :].astype(BF))
+                turned = block * cosine + swap_halves(block) * sines
+                if i == 0:
+                    turned = turned * (HD**-0.5 * math.log2(math.e))
+                put(ref, c, turned.astype(BF), slice(h * LANES, (h + 1) * LANES))
+            at = 2 * padded + h * LANES
+            block = mixture[:, at : at + LANES]
+            block = jnp.where(lane_of(block.shape) == HD, 1.0, block)
+            put(r.v, c, block.astype(BF), slice(h * LANES, (h + 1) * LANES))
         return carry
 
     lax.fori_loop(0, CHUNKS, project, 0)
@@ -592,29 +598,74 @@
 
     def attend(first, keys, kept):
         span = slice(first, first + rows)
-
-        def one_head(h, carry):
+        lane = lane_of((rows, LANES))
+        row, column = row_of((rows, rows)), lane_of((rows, rows))
+
+        def one_head(h, inverses):
             at = head_lanes(h)
-            scores = dot_right(r.q[span, at], r.k[0:keys, at])
-            key = lane_of((rows, keys))
-            allowed = (key <= row_of((rows, keys)) + first) | (key < prefix)
-            scores = jnp.where(allowed, scores, -1000000000.0)
-            powers = jnp.exp(scores - jnp.max(scores, axis=1, keepdims=True))
-            inverse = 1.0 / jnp.sum(powers, axis=1, keepdims=True)
-            weights = (powers * inverse).astype(BF)
-            kept[h] = weights
-            r.att[span, at] = dot(weights, r.v[0:keys, at]).astype(BF)
-            return carry
-
-        lax.fori_loop(0, heads, one_head, 0)
+            query = r.q[span, at]
+            tiles = []
+            for start in range(0, keys, rows):
+                scores = dot_right(query, r.k[start : start + rows, at])
+                allowed = None
+                if start == first:
+                    allowed = column <= row
+                if start + rows > first + 1 and start < PREFIX_MOST:
+                    in_prefix = column < prefix - start
+                    allowed = in_prefix if allowed is None else allowed | in_prefix
+                if allowed is not None:
+                    scores = jnp.where(allowed, scores, -1000000000.0)
+                tiles.append(scores)
+            highest = functools.reduce(jnp.maximum, tiles)
+            highest = jnp.max(highest, axis=1, keepdims=True)
+            total = jnp.zeros((rows, LANES), F32)
+            for j, scores in enumerate(tiles):
+                weights = jnp.exp2(scores - highest).astype(BF)
+                kept[h, :, j * rows : (j + 1) * rows] = weights
+                total = total + dot(weights, r.v[j * rows : (j + 1) * rows, at])
+            inverse = 1.0 / total[:, HD : HD + 1]
+            r.att[span, at] = jnp.where(lane < HD, total * inverse, 0.0).astype(BF)
+            return jnp.where(lane == h, inverse, inverses)
+
+        r.inverse[span] = lax.fori_loop(0, heads, one_head, jnp.zeros((rows, LANES), F32))
         r.part1[span] = dot(r.att[span], r.wop[...]).astype(BF)
 
-    for block in blocks:
-        attend(*block)
-    for c in range(CHUNKS):
-        scatter1.send(c)
-    for c in range(CHUNKS):
-        scatter1.middle(c)
+    def attend_step(step, carry):
+        core, side = lax.rem(p.t, 2), p.t // 2
+        side = side + (1 - step // 2) * (1 - 2 * side)
+        core = core + (1 - lax.rem(step, 2)) * (1 - 2 * core)
+        wanted = 2 * side + core
+        for i, block in enumerate(blocks):
+
+            @pl.when(wanted == i)
+            def _(block=block):
+                attend(*block)
+
+        @pl.when(lax.rem(step, 2) == 0)
+        def _():
+            for c in range(CHUNKS):
+                scatter1.near_copy(1 - step // 2, c).start()
+
+        @pl.when(step == 1)
+        def _():
+            for c in range(CHUNKS):
+                scatter1.middle(c)
+
+        return carry
+
+    lax.fori_loop(0, SPLIT, attend_step, 0)
+
+    waiting = []
+
+    def spread(name):
+        if z.inside:
+            spreads[name].send()
+            waiting.extend((name, step) for step in range(Spread.STEPS))
+
+    def pair_sums(count):
+        for name, step in waiting[:count]:
+            spreads[name].middle(step)
+        del waiting[:count]
 
     def second_norm(c, carry):
         span = scatter1.span(c)
@@ -644,22 +695,25 @@
         back = dot_right(gate_back, r.wgu[:, 0:units]) + dot_right(up_back, r.wgu[:, units:])
         put(r.part3, c, back.astype(BF))
         scatter3.send(c)
+
+        @pl.when(c > 0)
+        def _():
+            scatter3.middle(c - 1)
+
         return carry
 
     lax.fori_loop(0, CHUNKS, feed_forward, 0)
-    for c in range(CHUNKS):
-        scatter3.middle(c)
+    scatter3.middle(CHUNKS - 1)
 
     tile = 2 * LANES
 
     def gate_up_tile(j, carry):
         at = pl.ds(pl.multiple_of(j * tile, tile), tile)
-        r.gu_part[at] = dot(r.n2[:, at].T, r.gub[...]).astype(BF)
+        r.gu_part[at] = dot(r.n2[:, at].T, r.gub[0:length]).astype(BF)
         return carry
 
     lax.fori_loop(0, width // tile, gate_up_tile, 0)
-    if z.inside:
-        spreads["gu"].send()
+    spread("gu")
 
     r.sums[...] = jnp.zeros_like(r.sums)
 
@@ -698,12 +752,16 @@
         return carry
 
     lax.fori_loop(0, width // tile, down_tile, 0)
-    if z.inside:
-        spreads["dn"].send()
+    spread("dn")
+    pair_sums(2)
 
     def attended_back(c, carry):
         gather3.receive(c)
-        put(r.do, c, dot_right(take(r.ab, c), r.wop[...]).astype(BF))
+        back = dot_right(take(r.ab, c), r.wop[...])
+        inverse = take(r.inverse, c)
+        for h in range(heads):
+            at = slice(h * LANES, (h + 1) * LANES)
+            put(r.do, c, (back[:, at] * inverse[:, h : h + 1]).astype(BF), at)
         return carry
 
     lax.fori_loop(0, CHUNKS, attended_back, 0)
@@ -733,10 +791,12 @@
             r.dk[:, 0:keys] += key_back
             r.dv[:, 0:keys] += value_back
 
+    n1_turned, ab_turned = r.gub.at[0:width], r.wgu
+
     def turned_tile(j, carry):
         at = pl.ds(pl.multiple_of(j * tile, tile), tile)
-        r.n1t[at] = r.n1[:, at].T
-        r.abt[at] = r.ab[:, at].T
+        n1_turned[at] = r.n1[:, at].T
+        ab_turned[at] = r.ab[:, at].T
         return carry
 
     lax.fori_loop(0, width // tile, turned_tile, 0)
@@ -748,8 +808,8 @@
         def head_tile(j, carry):
             at = pl.ds(pl.multiple_of(j * tile, tile), tile)
             mixed = jnp.concatenate([r.mixb[:, span] for span in lanes], axis=1)
-            grad = dot(r.n1t[at], mixed)
-            outer = dot(r.abt[at], r.att[:, h * LANES : (h + 1) * LANES])
+            grad = dot(n1_turned[at], mixed)
+            outer = dot(ab_turned[at], r.att[:, h * LANES : (h + 1) * LANES])
             first = grad[:, :LANES] + roll64(grad[:, LANES : 2 * LANES])
             second = grad[:, 2 * LANES :] + roll64(outer)
             part[at, 0:LANES] = first.astype(BF)
@@ -758,45 +818,39 @@
 
         lax.fori_loop(0, width // tile, head_tile, 0)
 
-    waiting = [("gu", i) for i in range(1, z.groups + 1)] + [("dn", i) for i in range(1, z.groups + 1)]
-
-    def pair_sums(count):
-        for name, step in waiting[:count]:
-            if z.inside:
-                spreads[name].middle(step)
-        del waiting[:count]
-
-    pair_sums(2 * z.groups // 4)
+    pair_sums(1)
     for h in range(heads):
         for i in reversed(range(SPLIT)):
             first, keys, kept = blocks[i]
             attend_back(h, first, keys, kept, i == SPLIT - 1)
-            pair_sums(1)
         for i in range(SPLIT):
             span = slice(i * rows, (i + 1) * rows)
             at = padded + h * LANES
-            r.mixb[span, at : at + LANES] = unrotate(upright(r.dk[:, span]), span)
+            key_back = upright(r.dk[:, span]) * math.log(2.0)
+            r.mixb[span, at : at + LANES] = unrotate(key_back, span)
             at = 2 * padded + h * LANES
             r.mixb[span, at : at + LANES] = upright(r.dv[:, span]).astype(BF)
         if h < heads - 1:
             head_tiles(h)
-            if z.inside:
-                spreads[f"at{h}"].send()
-                waiting.extend((f"at{h}", i) for i in range(1, z.groups + 1))
+            spread(f"at{h}")
+            pair_sums(h + 1)
     scatter1.close()
 
     def first_norm_part(c, carry):
         put(r.part1, c, dot(take(r.mixb, c), r.wap[...]).astype(BF))
         scatter4.send(c)
+
+        @pl.when(c > 0)
+        def _():
+            scatter4.middle(c - 1)
+
         return carry
 
     lax.fori_loop(0, CHUNKS, first_norm_part, 0)
-    for c in range(CHUNKS):
-        scatter4.middle(c)
+    scatter4.middle(CHUNKS - 1)
     head_tiles(heads - 1)
-    if z.inside:
-        spreads[f"at{heads - 1}"].send()
-    pair_sums(len(waiting))
+    spread(f"at{heads - 1}")
+    pair_sums(max(0, len(waiting) - Spread.STEPS - 2))
 
     def block_out(c, carry):
         span = scatter2.span(c)
@@ -895,8 +949,7 @@
         for step in range(1, n):
             small_copy(step).start()
         r.sm_in[p.d] = r.sm_out[p.d]
-        for step in range(1, z.groups + 1):
-            spreads[f"at{heads - 1}"].middle(step)
+        pair_sums(len(waiting))
     for step in range(n):
         of = peer(step)
         pass_copy(1, of, True).wait_recv()

time: 155 us -> 139 us (0.90)
  Pallas kernels: 154 us -> 137 us
    pallas_call x1, Pallas kernels: 150 us -> 134 us  [shards(): pl.pallas_call(functools.partial(block_kernel, z, names), out_shape=[jax....]
where the time goes in v4:
time: 139 us
  Pallas kernels  137 us (99%)
    pallas_call x1, Pallas kernels, shards(): pl.pallas_call(functools.partial(block_kernel, z, names), out_shape=[jax....  134 us
    pallas_call x1, Pallas kernels, finish_outputs(): pl.pallas_call(functools.partial(finish_kernel, z, (*got, *outs)), out_sh...  3.75 us

profile of v4, /device:TPU:0, one launch (start us, length us, event | category | flops | bytes accessed | tf_op | source)
XLA Modules:
  0.0 138.6 jit_solution(15676921866313304722)
XLA Ops:
  1.3 133.5 %block.1 = (bf16[256,768]{1,0:T(8,128)(2,1)}, f32[256,768]{1,0:T(8,128)}, f32[512,384]{1,0:T(8,128)}, f32[96,1024]{1,0:T(8,128)}, f32[96,512]{1,0:T(8,128)}, /*i...) custom-call(bf16[256,768]{1,0:T(8,128)(2,1)} %refs_0_.1, s32[1,256]{1,0:T(1,128)} %bitcast.14, ...), custom_call_target="tpu_custom_call" | custom-call | tf_op jit(solution)/shard_map/block/pallas_call | solution.py:1091
  134.8 3.8 %finish.1 = (bf16[256,768]{1,0:T(8,128)(2,1)}, f32[256,768]{1,0:T(8,128)}, f32[192,512]{1,0:T(8,128)}, f32[192,512]{1,0:T(8,128)}, f32[24,384]{1,0:T(8,128)}, /*...) custom-call(bf16[256,768]{1,0:T(8,128)(2,1)} %get-tuple-element.33.r, ...), custom_call_target="tpu_custom_call" | custom-call | tf_op jit(solution)/shard_map/finish/pallas_call | solution.py:1049

commit v5 on v4

--- a/solution.py
+++ b/solution.py
@@ -253,6 +253,7 @@
         emb=vmem((rows, width), BF),
         ids=vmem((2 * n, 1, rows), jnp.int32),
         own_ids=vmem((2, 1, rows), jnp.int32),
+        pick=vmem((2, rows, z.slots), BF),
         table_b=vmem((z.table_width, z.table_rows), BF),
         table_t=vmem((z.table_width, z.table_rows), BF),
         nw=vmem((z.pair_width, width), BF),
@@ -265,7 +266,6 @@
         cot=vmem((length, width), BF),
         cosine=vmem((length, LANES), F32),
         sines=vmem((length, LANES), F32),
-        pick=vmem((2, rows, z.slots), BF),
         pick_t=vmem((2, z.slots, rows), BF),
         lids=vmem((SPLIT, 2, 8, z.slots), jnp.int32),
         rows_out=vmem((z.slots, z.pair_width), BF),
@@ -302,8 +302,8 @@
         id_sem=dma((2,)),
         row_sem=dma((2, n)),
         lid_sem=dma((2, 3)),
-        back_sem=dma((2, n)),
-        pass_sem=dma((6, n)),
+        back_sem=dma((2, 2 * n)),
+        pass_sem=dma((6, 2 * n)),
         ag1_sem=dma((chunks, 6)),
         ag2_sem=dma((chunks, 6)),
         ag3_sem=dma((chunks, 6)),
@@ -412,7 +412,7 @@
         src = r.output_weight.at[pl.ds(h * HD, HD)]
         loads.append((src, r.wop.at[pl.ds(h * LANES, HD)]))
     loads = [pltpu.make_async_copy(src, dst, r.in_sem.at[i]) for i, (src, dst) in enumerate(loads)]
-    for load in loads:
+    for load in loads[:4]:
         load.start()
 
     pl.semaphore_wait(barrier, n - 1 + 3)
@@ -429,6 +429,8 @@
     for step in range(1, n):
         for k in range(2):
             id_copy(step, k).start()
+    for load in loads[4:]:
+        load.start()
 
     lane = lane_of((32, LANES))
     low = jnp.where(lane < 32, lane, lane - 32)
@@ -449,16 +451,19 @@
     loads[1].wait()
     earlier = onehot(row_of((rows, rows)) < lane_of((rows, rows)))
     later = onehot(row_of((rows, rows)) > lane_of((rows, rows)))
+    lane = lane_of((rows, LANES))
+    start, half_cap = (lane * z.table_rows).astype(F32), cap // 2
     for k in range(2):
         r.ids[k * n + p.d] = r.own_ids[k]
-        own = jnp.broadcast_to(r.own_ids[k].astype(F32), (LANES, rows))
-        column = own.T
-        start = (lane_of((rows, LANES)) * z.table_rows).astype(F32)
+        column = jnp.broadcast_to(r.own_ids[k].astype(F32), (LANES, rows)).T
         held = (column >= start) & (column < start + z.table_rows)
         ranks = dot(later, onehot(held))
-        slot = jnp.where(held, ranks + (lane_of((rows, LANES)) * cap).astype(F32), 0.0)
+        slot = jnp.where(held, ranks + (lane * cap).astype(F32), 0.0)
         slot = jnp.sum(slot, axis=1, keepdims=True)
         r.pick[k] = onehot(slot.astype(jnp.int32) == lane_of((rows, slots)))
+        second = jnp.where(ranks >= half_cap, float((n - 1) * half_cap), 0.0)
+        slot = jnp.where(held, ranks + (lane * half_cap).astype(F32) + second, 0.0)
+        slot = jnp.sum(slot, axis=1, keepdims=True)
         across = jnp.broadcast_to(slot, (rows, LANES)).T[0:1]
         r.pick_t[k] = onehot(across.astype(jnp.int32) == row_of((slots, rows)))
 
@@ -488,8 +493,9 @@
             hit = tags[at : at + 1] == row_of((cap, rows))
             value = jnp.where(hit, local[at : at + 1], 0.0)
             columns.append(jnp.sum(value, axis=1, keepdims=True) - 1.0)
+        picked.append(jnp.concatenate(columns, axis=0).astype(jnp.int32))
+        columns = [item[:half_cap] for item in columns] + [item[half_cap:] for item in columns]
         column = jnp.concatenate(columns, axis=0)
-        picked.append(column.astype(jnp.int32))
         across = jnp.broadcast_to(column, (slots, LANES)).T[0:8]
         r.lids[p.t, k] = across.astype(jnp.int32)
     half = slots // 2
@@ -593,20 +599,16 @@
     probs = (r.probs0, r.probs1, r.probs2, r.probs3)
     blocks = [(i * rows, z.keys[i], probs[i]) for i in range(SPLIT)]
 
-    def head_lanes(h):
-        return pl.ds(pl.multiple_of(h * LANES, LANES), LANES)
-
     def attend(first, keys, kept):
         span = slice(first, first + rows)
         lane = lane_of((rows, LANES))
         row, column = row_of((rows, rows)), lane_of((rows, rows))
 
-        def one_head(h, inverses):
-            at = head_lanes(h)
-            query = r.q[span, at]
+        def score_tiles(h):
+            at = slice(h * LANES, (h + 1) * LANES)
             tiles = []
             for start in range(0, keys, rows):
-                scores = dot_right(query, r.k[start : start + rows, at])
+                scores = dot_right(r.q[span, at], r.k[start : start + rows, at])
                 allowed = None
                 if start == first:
                     allowed = column <= row
@@ -616,18 +618,26 @@
                 if allowed is not None:
                     scores = jnp.where(allowed, scores, -1000000000.0)
                 tiles.append(scores)
-            highest = functools.reduce(jnp.maximum, tiles)
-            highest = jnp.max(highest, axis=1, keepdims=True)
+            return tiles
+
+        inverses = jnp.zeros((rows, LANES), F32)
+        every = [score_tiles(h) for h in range(heads)]
+        tops = [jnp.max(functools.reduce(jnp.maximum, tiles), axis=1, keepdims=True) for tiles in every]
+        totals = []
+        for h in range(heads):
+            at = slice(h * LANES, (h + 1) * LANES)
             total = jnp.zeros((rows, LANES), F32)
-            for j, scores in enumerate(tiles):
-                weights = jnp.exp2(scores - highest).astype(BF)
+            for j, scores in enumerate(every[h]):
+                weights = jnp.exp2(scores - tops[h]).astype(BF)
                 kept[h, :, j * rows : (j + 1) * rows] = weights
                 total = total + dot(weights, r.v[j * rows : (j + 1) * rows, at])
+            totals.append(total)
+        for h, total in enumerate(totals):
+            at = slice(h * LANES, (h + 1) * LANES)
             inverse = 1.0 / total[:, HD : HD + 1]
             r.att[span, at] = jnp.where(lane < HD, total * inverse, 0.0).astype(BF)
-            return jnp.where(lane == h, inverse, inverses)
-
-        r.inverse[span] = lax.fori_loop(0, heads, one_head, jnp.zeros((rows, LANES), F32))
+            inverses = jnp.where(lane == h, inverse, inverses)
+        r.inverse[span] = inverses
         r.part1[span] = dot(r.att[span], r.wop[...]).astype(BF)
 
     def attend_step(step, carry):
@@ -743,6 +753,7 @@
         return carry
 
     lax.fori_loop(0, CHUNKS, branch_two, 0)
+    pair_sums(0)
     for c in range(CHUNKS):
         scatter2.middle(c)
 
@@ -805,18 +816,13 @@
         part = getattr(r, f"at{h}_part")
         lanes = [slice(c * padded + h * LANES, c * padded + (h + 1) * LANES) for c in range(3)]
 
-        def head_tile(j, carry):
-            at = pl.ds(pl.multiple_of(j * tile, tile), tile)
-            mixed = jnp.concatenate([r.mixb[:, span] for span in lanes], axis=1)
-            grad = dot(n1_turned[at], mixed)
-            outer = dot(ab_turned[at], r.att[:, h * LANES : (h + 1) * LANES])
-            first = grad[:, :LANES] + roll64(grad[:, LANES : 2 * LANES])
-            second = grad[:, 2 * LANES :] + roll64(outer)
-            part[at, 0:LANES] = first.astype(BF)
-            part[at, LANES:] = second.astype(BF)
-            return carry
-
-        lax.fori_loop(0, width // tile, head_tile, 0)
+        mixed = jnp.concatenate([r.mixb[:, span] for span in lanes], axis=1)
+        grad = dot(n1_turned[...], mixed)
+        outer = dot(ab_turned[...], r.att[:, h * LANES : (h + 1) * LANES])
+        first = grad[:, :LANES] + roll64(grad[:, LANES : 2 * LANES])
+        second = grad[:, 2 * LANES :] + roll64(outer)
+        part[:, 0:LANES] = first.astype(BF)
+        part[:, LANES:] = second.astype(BF)
 
     pair_sums(1)
     for h in range(heads):
@@ -833,7 +839,7 @@
         if h < heads - 1:
             head_tiles(h)
             spread(f"at{h}")
-            pair_sums(h + 1)
+            pair_sums((1, 2)[h])
     scatter1.close()
 
     def first_norm_part(c, carry):
@@ -848,9 +854,10 @@
 
     lax.fori_loop(0, CHUNKS, first_norm_part, 0)
     scatter4.middle(CHUNKS - 1)
+    pair_sums(4)
     head_tiles(heads - 1)
     spread(f"at{heads - 1}")
-    pair_sums(max(0, len(waiting) - Spread.STEPS - 2))
+    pair_sums(4)
 
     def block_out(c, carry):
         span = scatter2.span(c)
@@ -875,29 +882,37 @@
     low_table = lane_of((slots, z.pair_width)) < z.table_width
     outgoing = jnp.where(low_table, dot(r.pick_t[0], row_back), dot(r.pick_t[1], row_back))
     r.back_out[...] = outgoing.astype(BF)
-
-    def back_slots(block, of):
-        return r.back_in.at[pl.ds(pl.multiple_of(block * slots + of * cap, cap), cap)]
-
-    def back_copy(step, incoming=False):
+    pair_sums(0)
+
+    def slots_of(block, turn, of):
+        start = block * slots + (turn * n + of) * half_cap
+        return pl.ds(pl.multiple_of(start, half_cap), half_cap)
+
+    def back_copy(step, turn, incoming=False):
         to = peer(step)
-        src = r.back_out.at[pl.ds(pl.multiple_of(to * cap, cap), cap)]
-        dst = back_slots(p.t, to if incoming else p.d)
-        recv = r.back_sem.at[1, to if incoming else p.d]
-        return make_copy(src, dst, r.back_sem.at[0, 0], recv, dp=to)
-
-    def pass_copy(kind, of, incoming=False):
+        of = to if incoming else p.d
+        return make_copy(
+            r.back_out.at[slots_of(0, turn, to)],
+            r.back_in.at[slots_of(p.t, turn, of)],
+            r.back_sem.at[0, 0],
+            r.back_sem.at[1, turn * n + of],
+            dp=to,
+        )
+
+    def pass_copy(kind, turn, of, incoming=False):
         block = ((p.t, p.t1), (p.t, p.t2), (p.t2, p.t3))[kind][1 if incoming else 0]
-        ref = back_slots(block, of)
+        ref = r.back_in.at[slots_of(block, turn, of)]
+        at = turn * n + of
         target = p.t2 if kind == 1 else p.t1
         return make_copy(
-            ref, ref, r.pass_sem.at[2 * kind, of], r.pass_sem.at[2 * kind + 1, of], tensor=target
+            ref, ref, r.pass_sem.at[2 * kind, at], r.pass_sem.at[2 * kind + 1, at], tensor=target
         )
 
-    for step in range(1, n):
-        back_copy(n - step).start()
-    own_block = pl.ds(pl.multiple_of(p.t * slots + p.d * cap, cap), cap)
-    r.back_in[own_block] = r.back_out[own_slots]
+    for turn in range(2):
+        for step in range(1, n):
+            back_copy(n - step, turn).start()
+    for turn in range(2):
+        r.back_in[slots_of(p.t, turn, p.d)] = r.back_out[slots_of(0, turn, p.d)]
 
     gains = jnp.concatenate(
         [r.sums[0, 0:1], r.sums[1, 0:1], jnp.zeros((LANES - 2, width), F32)], axis=0
@@ -935,12 +950,12 @@
     else:
         r.sm_total[...] = small
 
-    pass_copy(0, p.d).start()
-    pass_copy(1, p.d).start()
-    for step in range(1, n):
-        back_copy(step, True).wait_recv()
-        pass_copy(1, peer(step)).start()
-        pass_copy(0, peer(step)).start()
+    for turn in range(2):
+        for step in range(n):
+            if step > 0:
+                back_copy(step, turn, True).wait_recv()
+            pass_copy(1, turn, peer(step)).start()
+            pass_copy(0, turn, peer(step)).start()
     if z.inside:
         small_near(0).wait_recv()
         small_far.wait_recv()
@@ -949,11 +964,12 @@
         for step in range(1, n):
             small_copy(step).start()
         r.sm_in[p.d] = r.sm_out[p.d]
-        pair_sums(len(waiting))
-    for step in range(n):
-        of = peer(step)
-        pass_copy(1, of, True).wait_recv()
-        pass_copy(2, of).start()
+        pair_sums(6)
+    for turn in range(2):
+        for step in range(n):
+            of = peer(step)
+            pass_copy(1, turn, of, True).wait_recv()
+            pass_copy(2, turn, of).start()
     for i in range(3):
         lid_copy(i, True).wait_recv()
     kept = z.table_rows // SPLIT
@@ -971,12 +987,15 @@
             r.table_grads[:, at] = value if fresh else r.table_grads[:, at] + value
 
     add_rows(p.t, True)
-    for step in range(n):
-        pass_copy(0, peer(step), True).wait_recv()
+    for turn in range(2):
+        for step in range(n):
+            pass_copy(0, turn, peer(step), True).wait_recv()
     add_rows(p.t1)
     add_rows(p.t2)
-    for step in range(n):
-        pass_copy(2, peer(step), True).wait_recv()
+    pair_sums(99)
+    for turn in range(2):
+        for step in range(n):
+            pass_copy(2, turn, peer(step), True).wait_recv()
     add_rows(p.t3)
 
     if z.inside:
@@ -1005,9 +1024,10 @@
         small_near(0).wait_send()
         small_near(1).wait_send()
         small_far.wait_send()
-    for step in range(n):
-        for kind in range(3):
-            pass_copy(kind, peer(step)).wait_send()
+    for kind in range(3):
+        for turn in range(2):
+            for step in range(n):
+                pass_copy(kind, turn, peer(step)).wait_send()
 
 
 def finish_kernel(z, names, *refs):

time: 139 us -> 136 us (0.978)
  Pallas kernels: 137 us -> 134 us
    pallas_call x1, Pallas kernels: 134 us -> 130 us  [shards(): pl.pallas_call(functools.partial(block_kernel, z, names), out_shape=[jax....]
where the time goes in v5:
time: 136 us; the launch traced here: 135 us
  Pallas kernels  134 us (99%)
    pallas_call x1, Pallas kernels, shards(): pl.pallas_call(functools.partial(block_kernel, z, names), out_shape=[jax....  130 us
    pallas_call x1, Pallas kernels, finish_outputs(): pl.pallas_call(functools.partial(finish_kernel, z, (*got, *outs)), out_sh...  3.75 us

profile of v5, /device:TPU:0, one launch (start us, length us, event | category | flops | bytes accessed | tf_op | source)
XLA Modules:
  0.0 135.4 jit_solution(1492997141383368107)
XLA Ops:
  1.3 130.3 %block.1 = (bf16[256,768]{1,0:T(8,128)(2,1)}, f32[256,768]{1,0:T(8,128)}, f32[512,384]{1,0:T(8,128)}, f32[96,1024]{1,0:T(8,128)}, f32[96,512]{1,0:T(8,128)}, /*i...) custom-call(bf16[256,768]{1,0:T(8,128)(2,1)} %refs_0_.1, s32[1,256]{1,0:T(1,128)} %bitcast.14, ...), custom_call_target="tpu_custom_call" | custom-call | tf_op jit(solution)/shard_map/block/pallas_call | solution.py:1111
  131.6 3.8 %finish.1 = (bf16[256,768]{1,0:T(8,128)(2,1)}, f32[256,768]{1,0:T(8,128)}, f32[192,512]{1,0:T(8,128)}, f32[192,512]{1,0:T(8,128)}, f32[24,384]{1,0:T(8,128)}, /*...) custom-call(bf16[256,768]{1,0:T(8,128)(2,1)} %get-tuple-element.33.r, ...), custom_call_target="tpu_custom_call" | custom-call | tf_op jit(solution)/shard_map/finish/pallas_call | solution.py:1069

commit v6 on v5

--- a/solution.py
+++ b/solution.py
@@ -177,34 +177,41 @@
 class Spread:
     STEPS = 4
 
-    def __init__(self, z, pos, part, pair_in, next_out, next_in, out, sems):
+    def __init__(self, z, pos, axes, part, pair_in, next_out, next_in, out, sems):
         self.z, self.pos, self.part, self.pair_in = z, pos, part, pair_in
         self.next_out, self.next_in, self.out, self.sems = next_out, next_in, out, sems
-        near = pos.place + 1 - 2 * lax.rem(pos.place, 2)
-        far = lax.rem(pos.place + 2, 4)
-        both = lax.rem(near + 2, 4)
-        self.order = (both, near, far, pos.place)
+        self.axes = axes
+        self.order = (axes[1:], axes[1:2], axes[2:], ())
+
+    def across(self, axes):
+        place, parity = self.pos.place, self.pos.parity
+        if "near" in axes:
+            place = place + 1 - 2 * lax.rem(place, 2)
+        if "far" in axes:
+            place = lax.rem(place + 2, 4)
+        if "x" in axes:
+            parity = 1 - parity
+        return 2 * place + parity
 
     def rows(self, peer):
         return pl.ds(pl.multiple_of(peer * self.z.piece, self.z.piece), self.z.piece)
 
     def pair_copy(self, step):
         return make_copy(
-            self.part.at[self.rows(self.order[step] * 2 + 1 - self.pos.parity)],
+            self.part.at[self.rows(self.across(self.axes[:1] + self.order[step]))],
             self.pair_in.at[step],
             self.sems.at[0, step],
             self.sems.at[1, step],
-            dp=self.pos.partner,
+            dp=self.across(self.axes[:1]),
         )
 
     def next_copy(self, step):
-        place = self.order[1] if step < 2 else self.order[2]
         return make_copy(
             self.next_out.at[step],
             self.next_in.at[step],
             self.sems.at[2, step],
             self.sems.at[3, step],
-            dp=place * 2 + self.pos.parity,
+            dp=self.across(self.axes[1:2] if step < 2 else self.axes[2:]),
         )
 
     def send(self):
@@ -213,7 +220,7 @@
 
     def middle(self, step):
         self.pair_copy(step).wait_recv()
-        own = self.part[self.rows(self.order[step] * 2 + self.pos.parity)].astype(F32)
+        own = self.part[self.rows(self.across(self.order[step]))].astype(F32)
         total = own + self.pair_in[step].astype(F32)
         if step >= 2:
             self.next_copy(step - 2).wait_recv()
@@ -243,7 +250,6 @@
         self.t2 = self.t + 2 - 4 * side
         self.t3 = self.t1 + 2 - 4 * side
         self.parity, self.place = lax.rem(self.d, 2), self.d // 2
-        self.partner = self.d + 1 - 2 * self.parity
 
 
 def scratch_of(z):
@@ -317,7 +323,7 @@
     shapes["rs4_sem"] = dma((chunks, 6))
     if z.inside:
         heads = [(f"at{h}", z.attn_lanes) for h in range(z.heads)]
-        for name, lanes in (("gu", 2 * z.units), ("dn", z.units), *heads):
+        for name, lanes in (("ga", z.units), ("up", z.units), ("dn", z.units), *heads):
             shapes[f"{name}_part"] = vmem((width, lanes), BF)
             shapes[f"{name}_pair_in"] = vmem((4, z.piece, lanes), BF)
             shapes[f"{name}_next_out"] = vmem((3, z.piece, lanes), BF)
@@ -343,13 +349,15 @@
         table_grads=((z.table_rows // SPLIT, z.pair_width), F32),
     )
     if z.inside:
-        shapes["gu_out"] = ((z.piece, 2 * z.units), F32)
+        shapes["ga_out"] = ((z.piece, z.units), F32)
+        shapes["up_out"] = ((z.piece, z.units), F32)
         shapes["dn_out"] = ((z.piece, z.units), F32)
         for h in range(z.heads):
             shapes[f"at{h}_out"] = ((z.piece, z.attn_lanes), F32)
         shapes["sm_total"] = ((z.small, z.small_lanes), F32)
     else:
-        shapes["gu_part"] = ((width, 2 * z.units), BF)
+        shapes["ga_part"] = ((width, z.units), BF)
+        shapes["up_part"] = ((width, z.units), BF)
         shapes["dn_part"] = ((width, z.units), BF)
         for h in range(z.heads):
             shapes[f"at{h}_part"] = ((width, z.attn_lanes), BF)
@@ -375,9 +383,10 @@
     scatter1, scatter2, scatter3, scatter4 = scatters
     spreads = {}
     if z.inside:
-        for name in ("gu", "dn", *(f"at{h}" for h in range(heads))):
+        for name in ("ga", "up", "dn", *(f"at{h}" for h in range(heads))):
+            axes = ("near", "far", "x") if name == "ga" else ("x", "near", "far")
             spreads[name] = Spread(
-                z, p, getattr(r, f"{name}_part"), getattr(r, f"{name}_pair_in"),
+                z, p, axes, getattr(r, f"{name}_part"), getattr(r, f"{name}_pair_in"),
                 getattr(r, f"{name}_next_out"), getattr(r, f"{name}_next_in"),
                 getattr(r, f"{name}_out"), getattr(r, f"{name}_sem"),
             )
@@ -719,11 +728,16 @@
 
     def gate_up_tile(j, carry):
         at = pl.ds(pl.multiple_of(j * tile, tile), tile)
-        r.gu_part[at] = dot(r.n2[:, at].T, r.gub[0:length]).astype(BF)
+        both = dot(r.n2[:, at].T, r.gub[0:length]).astype(BF)
+        r.ga_part[at] = both[:, :units]
+        r.up_part[at] = both[:, units:]
         return carry
 
     lax.fori_loop(0, width // tile, gate_up_tile, 0)
-    spread("gu")
+    if z.inside:
+        spreads["ga"].send()
+        spreads["up"].send()
+        waiting.extend((name, step) for step in range(Spread.STEPS) for name in ("ga", "up"))
 
     r.sums[...] = jnp.zeros_like(r.sums)
 
@@ -747,13 +761,13 @@
 
     lax.fori_loop(0, CHUNKS, second_back, 0)
 
+
     def branch_two(c, carry):
         put(r.part2, c, dot(take(r.act, c), r.wd[...]).astype(BF))
         scatter2.send(c)
         return carry
 
     lax.fori_loop(0, CHUNKS, branch_two, 0)
-    pair_sums(0)
     for c in range(CHUNKS):
         scatter2.middle(c)
 
@@ -764,7 +778,7 @@
 
     lax.fori_loop(0, width // tile, down_tile, 0)
     spread("dn")
-    pair_sums(2)
+    pair_sums(4)
 
     def attended_back(c, carry):
         gather3.receive(c)
@@ -824,7 +838,6 @@
         part[:, 0:LANES] = first.astype(BF)
         part[:, LANES:] = second.astype(BF)
 
-    pair_sums(1)
     for h in range(heads):
         for i in reversed(range(SPLIT)):
             first, keys, kept = blocks[i]
@@ -839,7 +852,7 @@
         if h < heads - 1:
             head_tiles(h)
             spread(f"at{h}")
-            pair_sums((1, 2)[h])
+            pair_sums((4, 2)[h])
     scatter1.close()
 
     def first_norm_part(c, carry):
@@ -854,10 +867,10 @@
 
     lax.fori_loop(0, CHUNKS, first_norm_part, 0)
     scatter4.middle(CHUNKS - 1)
-    pair_sums(4)
+    pair_sums(3)
     head_tiles(heads - 1)
     spread(f"at{heads - 1}")
-    pair_sums(4)
+    pair_sums(5)
 
     def block_out(c, carry):
         span = scatter2.span(c)
@@ -882,7 +895,6 @@
     low_table = lane_of((slots, z.pair_width)) < z.table_width
     outgoing = jnp.where(low_table, dot(r.pick_t[0], row_back), dot(r.pick_t[1], row_back))
     r.back_out[...] = outgoing.astype(BF)
-    pair_sums(0)
 
     def slots_of(block, turn, of):
         start = block * slots + (turn * n + of) * half_cap
@@ -1040,8 +1052,8 @@
     gains = r.sm_total[:, z.pair_width :]
     r.first[...] = gains[:, 0:1].T
     r.second[...] = gains[:, 1:2].T
-    r.gate[...] = r.gu_out[:, : z.units]
-    r.up[...] = r.gu_out[:, z.units :]
+    r.gate[...] = r.ga_out[...]
+    r.up[...] = r.up_out[...]
     r.down[...] = r.dn_out[...]
     side = 3 * HD
     for h in range(z.heads):
@@ -1141,7 +1153,7 @@
         def summed(part, axes):
             return lax.psum_scatter(part, axes, scatter_dimension=0, tiled=True)
 
-        for name in ("gu", "dn", *(f"at{h}" for h in range(heads))):
+        for name in ("ga", "up", "dn", *(f"at{h}" for h in range(heads))):
             got[f"{name}_out"] = summed(got.pop(f"{name}_part").astype(F32), "dp")
         got["sm_total"] = summed(got["sm_total"], ("dp", "tensor"))
     return finish_outputs(z, got)

time: 136 us -> 135 us (level)
  no operation moved by 1% of the time
where the time goes in v6:
time: 135 us
  Pallas kernels  133 us (99%)
  between operations  1.38 us (1%)
    pallas_call x1, Pallas kernels, shards(): pl.pallas_call(functools.partial(block_kernel, z, names), out_shape=[jax....  130 us
    pallas_call x1, Pallas kernels, finish_outputs(): pl.pallas_call(functools.partial(finish_kernel, z, (*got, *outs)), out_sh...  3.73 us

profile of v6, /device:TPU:0, one launch (start us, length us, event | category | flops | bytes accessed | tf_op | source)
XLA Modules:
  0.0 134.8 jit_solution(10505885056748495914)
XLA Ops:
  1.3 129.7 %block.1 = (bf16[256,768]{1,0:T(8,128)(2,1)}, f32[256,768]{1,0:T(8,128)}, f32[512,384]{1,0:T(8,128)}, f32[96,512]{1,0:T(8,128)}, f32[96,512]{1,0:T(8,128)}, /*in...) custom-call(bf16[256,768]{1,0:T(8,128)(2,1)} %refs_0_.1, ...), custom_call_target="tpu_custom_call" | custom-call | tf_op jit(solution)/shard_map/block/pallas_call | solution.py:1123
  131.0 3.7 %finish.1 = (bf16[256,768]{1,0:T(8,128)(2,1)}, f32[256,768]{1,0:T(8,128)}, f32[192,512]{1,0:T(8,128)}, f32[192,512]{1,0:T(8,128)}, f32[24,384]{1,0:T(8,128)}, /*...) custom-call(bf16[256,768]{1,0:T(8,128)(2,1)} %get-tuple-element.34.r, ...), custom_call_target="tpu_custom_call" | custom-call | tf_op jit(solution)/shard_map/finish/pallas_call | solution.py:1081

commit v7 on v6

--- a/solution.py
+++ b/solution.py
@@ -780,6 +780,15 @@
     spread("dn")
     pair_sums(4)
 
+    n1_turned, ab_turned = r.gub.at[0:width], r.wgu
+
+    def turned_tokens(j, carry):
+        at = pl.ds(pl.multiple_of(j * tile, tile), tile)
+        n1_turned[at] = r.n1[:, at].T
+        return carry
+
+    lax.fori_loop(0, width // tile, turned_tokens, 0)
+
     def attended_back(c, carry):
         gather3.receive(c)
         back = dot_right(take(r.ab, c), r.wop[...])
@@ -816,15 +825,12 @@
             r.dk[:, 0:keys] += key_back
             r.dv[:, 0:keys] += value_back
 
-    n1_turned, ab_turned = r.gub.at[0:width], r.wgu
-
-    def turned_tile(j, carry):
+    def turned_grads(j, carry):
         at = pl.ds(pl.multiple_of(j * tile, tile), tile)
-        n1_turned[at] = r.n1[:, at].T
         ab_turned[at] = r.ab[:, at].T
         return carry
 
-    lax.fori_loop(0, width // tile, turned_tile, 0)
+    lax.fori_loop(0, width // tile, turned_grads, 0)
 
     def head_tiles(h):
         part = getattr(r, f"at{h}_part")

time: 135 us -> 135 us (level)
  no operation moved by 1% of the time
where the time goes in v7:
time: 135 us
  Pallas kernels  134 us (99%)
  between operations  1.38 us (1%)
    pallas_call x1, Pallas kernels, shards(): pl.pallas_call(functools.partial(block_kernel, z, names), out_shape=[jax....  130 us
    pallas_call x1, Pallas kernels, finish_outputs(): pl.pallas_call(functools.partial(finish_kernel, z, (*got, *outs)), out_sh...  3.73 us

profile of v7, /device:TPU:0, one launch (start us, length us, event | category | flops | bytes accessed | tf_op | source)
XLA Modules:
  0.0 135.1 jit_solution(12546390634487539269)
XLA Ops:
  1.3 130.0 %block.1 = (bf16[256,768]{1,0:T(8,128)(2,1)}, f32[256,768]{1,0:T(8,128)}, f32[512,384]{1,0:T(8,128)}, f32[96,512]{1,0:T(8,128)}, f32[96,512]{1,0:T(8,128)}, /*in...) custom-call(bf16[256,768]{1,0:T(8,128)(2,1)} %refs_0_.1, ...), custom_call_target="tpu_custom_call" | custom-call | tf_op jit(solution)/shard_map/block/pallas_call | solution.py:1129
  131.3 3.7 %finish.1 = (bf16[256,768]{1,0:T(8,128)(2,1)}, f32[256,768]{1,0:T(8,128)}, f32[192,512]{1,0:T(8,128)}, f32[192,512]{1,0:T(8,128)}, f32[24,384]{1,0:T(8,128)}, /*...) custom-call(bf16[256,768]{1,0:T(8,128)(2,1)} %get-tuple-element.34.r, ...), custom_call_target="tpu_custom_call" | custom-call | tf_op jit(solution)/shard_map/finish/pallas_call | solution.py:1087
